TPU v7x, 32 devices: a whole 2x2x4 slice. The times are simulated.
32 devices in a mesh: tx: 8 (over z, x), ty: 4 (over y, core).
Axes of the slice: x: 2, y: 2, z: 4, core: 2. Of those that a mesh axis runs over, the one named last changes fastest.
Arguments:
- dynamics_residual: float32 [6, 48, 48, 16], P(None, 'tx', 'ty'), may hold values from -6 to 6
- density: float32 [6, 48, 48, 16], P(None, 'tx', 'ty'), may hold values from 0.5 to 8
- diagonal_gain: float32 [6, 48, 48, 16], P(None, 'tx', 'ty'), may hold values from 0.05 to 2
- vertical_coupling: float32 [6, 48, 48, 16], P(None, 'tx', 'ty'), may hold values from 0.2 to 8
- edge_panel: int32 [6, 4], replicated, may hold values from 0 to 5, as said below
- edge_side: int32 [6, 4], replicated, may hold values from 0 to 3, as said below
- edge_flip: int32 [6, 4], replicated, may hold values from 0 to 1, as said below
Outputs:
- solution: float32 [6, 48, 48, 16], P(None, 'tx', 'ty')
- coarse_correction: float32 [6, 24, 24, 16], P(None, 'tx', 'ty')
Inputs may be any that keep to these rules, and one draw needn't show every extreme that they name: The six panels are the faces of a cube, each with its own orientation and label: side s of panel p borders side edge_side[p, s] of panel edge_panel[p, s], the pairing is mutual, and no side borders a side of its own panel. `edge_side`: see edge_panel. `edge_flip`: equal on both sides of a bordering pair.
All inputs are finite; a program needn't handle non-finite values.
Results may differ from a plain program's by a relative error of at most 0.00005.
Values sent between devices are 32-bit elements; how exact they have to be, the bound alone decides.
A program may use at most 64 MiB of HBM per device.

v0:
```python
import functools

import jax
import jax.numpy as jnp
from jax import lax
from jax.experimental import pallas as pl
from jax.experimental.pallas import tpu as pltpu
from jax.sharding import PartitionSpec as P

MESH = pl.DeviceIdType.MESH
relaxation = 0.8
LANES = 128


def round_up(value, unit):
    return (value + unit - 1) // unit * unit


def kernel(
    nr,
    nc,
    res_hbm,
    den_hbm,
    gain_hbm,
    vert_hbm,
    panel_ref,
    side_ref,
    flip_ref,
    spread,
    small_ref,
    inp,
    packed,
    st_row,
    st_col,
    nb_row,
    nb_col,
    rx_row,
    rx_col,
    in_sem,
    send_sem,
    nb_sem,
    row_sem,
    col_sem,
):
    _, panels, rows, cols, levels = inp.shape
    half_r, half_c = rows // 2, cols // 2
    k = cols // rows
    height = spread.shape[1] // 2
    r = lax.axis_index("tx")
    c = lax.axis_index("ty")
    is_row = (r == 0) | (r == nr - 1)
    is_col = (c == 0) | (c == nc - 1)
    tr = r // (nr - 1)
    tc = c // (nc - 1)

    def messages(n):
        found = []
        for i in range(k):
            src = st_row.at[n, tr, i]
            for f in range(2):
                slot = 4 * f + tr
                i_dst = i if f == 0 else k - 1 - i
                c_dst = c if f == 0 else nc - 1 - c
                r_dst = k * c + i if f == 0 else nr - 1 - k * c - i
                for e in range(2):
                    found.append(
                        (
                            is_row,
                            (e * (nr - 1), c_dst),
                            src,
                            rx_row.at[n, slot, i_dst],
                            row_sem.at[n, slot, i_dst],
                        )
                    )
                    found.append(
                        (
                            is_row,
                            (r_dst, e * (nc - 1)),
                            src,
                            rx_col.at[n, slot],
                            col_sem.at[n, slot],
                        )
                    )
        src = st_col.at[n, tc]
        for f in range(2):
            slot = 4 * f + 2 + tc
            g = r if f == 0 else nr - 1 - r
            for e in range(2):
                found.append(
                    (
                        is_col,
                        (e * (nr - 1), g // k),
                        src,
                        rx_row.at[n, slot, g % k],
                        row_sem.at[n, slot, g % k],
                    )
                )
                found.append(
                    (is_col, (g, e * (nc - 1)), src, rx_col.at[n, slot], col_sem.at[n, slot])
                )
        found.append((r > 0, (r - 1, c), st_row.at[n, 0], nb_row.at[n, 1], nb_sem.at[n, 1]))
        found.append((r < nr - 1, (r + 1, c), st_row.at[n, 1], nb_row.at[n, 0], nb_sem.at[n, 0]))
        found.append((c > 0, (r, c - 1), st_col.at[n, 0], nb_col.at[n, 1], nb_sem.at[n, 3]))
        found.append((c < nc - 1, (r, c + 1), st_col.at[n, 1], nb_col.at[n, 0], nb_sem.at[n, 2]))
        return found

    def same(dest):
        return (dest[0] == r) & (dest[1] == c)

    barrier = pltpu.get_barrier_semaphore()
    expected = jnp.int32(0)
    for active, dest, _, _, _ in messages(0):
        go = active & jnp.logical_not(same(dest))
        expected = expected + go.astype(jnp.int32)

        @pl.when(go)
        def _():
            pl.semaphore_signal(barrier, inc=1, device_id=dest, device_id_type=MESH)

    loads = [
        pltpu.make_async_copy(source, inp.at[i], in_sem.at[i])
        for i, source in enumerate((den_hbm, res_hbm, gain_hbm, vert_hbm))
    ]
    for load in loads:
        load.start()

    lane = lax.broadcasted_iota(jnp.int32, (height, LANES), 1)
    sub = lax.broadcasted_iota(jnp.int32, (height, LANES), 0)
    level = lane % levels
    first_level = level == 0
    last_level = level == levels - 1

    def lower(x):
        return jnp.where(first_level, 0.0, pltpu.roll(x, 1, 1))

    def upper(x):
        return jnp.where(last_level, 0.0, pltpu.roll(x, LANES - 1, 1))

    seg_h = st_col.shape[2]
    seg_lane = lax.broadcasted_iota(jnp.int32, (seg_h, LANES), 1)

    def pick_tables(side):
        index = seg_lane
        code = jnp.zeros_like(seg_lane)
        for p in range(panels):
            here = seg_lane // levels == p
            index = jnp.where(here, panel_ref[side, p] * levels + seg_lane % levels, index)
            code = jnp.where(here, flip_ref[side, p] * 4 + side_ref[side, p], code)
        return index, code

    row_pick = pick_tables(tr)
    col_pick = pick_tables(2 + tc)

    for load in loads:
        load.wait()

    def pack(value):
        filler = jnp.zeros((rows, cols, LANES - panels * levels), jnp.float32)
        return jnp.concatenate([value[p] for p in range(panels)] + [filler], axis=-1)

    def split(which, value):
        packed[which, :, :cols, :] = value
        if packed.shape[2] > cols:
            packed[which, :, cols:, :] = jnp.zeros(
                (rows, packed.shape[2] - cols, LANES), jnp.float32
            )
        return [
            [packed[which, y, pl.ds(b, height, stride=2), :] for b in range(2)]
            for y in range(rows)
        ]

    every = [(y, b) for y in range(rows) for b in range(2)]

    def fine(fun):
        return [[fun(y, b) for b in range(2)] for y in range(rows)]

    right_side = split(0, pack(inp[0] * inp[1]))
    gain = split(1, pack(inp[2]))
    vertical = split(2, pack(inp[3]))
    low_vert = fine(lambda y, b: lower(vertical[y][b]))
    inverse = fine(
        lambda y, b: relaxation / (gain[y][b] + 4.0 + vertical[y][b] + low_vert[y][b])
    )
    smoothed = fine(lambda y, b: inverse[y][b] * right_side[y][b])

    def start(n):
        for m, (active, dest, src, dst, sem) in enumerate(messages(n)):
            mine = same(dest)

            @pl.when(active & jnp.logical_not(mine))
            def _():
                pltpu.make_async_remote_copy(
                    src_ref=src,
                    dst_ref=dst,
                    send_sem=send_sem.at[n, m],
                    recv_sem=sem,
                    device_id=dest,
                    device_id_type=MESH,
                ).start()

            if m < 8 * k + 8:

                @pl.when(active & mine)
                def _():
                    pltpu.make_async_copy(src, dst, sem).start()

    def finish_sends(n):
        for m, (active, dest, src, dst, sem) in enumerate(messages(n)):

            @pl.when(active & jnp.logical_not(same(dest)))
            def _():
                pltpu.make_async_copy(src, src, send_sem.at[n, m]).wait()

    def mirrored(x, length):
        lines = [x[length - 1 - s : length - s] for s in range(length)]
        if seg_h > length:
            lines.append(jnp.zeros((seg_h - length, LANES), jnp.float32))
        return jnp.concatenate(lines, axis=0)

    def select(read, pick, length):
        index, code = pick
        parts = []
        for f in range(2):
            taken = jnp.zeros((seg_h, LANES), jnp.float32)
            for t in range(4):
                moved = jnp.take_along_axis(
                    read(4 * f + t), index, axis=1, mode="promise_in_bounds"
                )
                taken = jnp.where(code == 4 * f + t, moved, taken)
            parts.append(taken)
        return jnp.where(code >= 4, mirrored(parts[1], length), parts[0])

    def receive(n, length):
        def arrived(ref, sem):
            pltpu.make_async_copy(ref, ref, sem).wait()

        @pl.when(r > 0)
        def _():
            arrived(nb_row.at[n, 0], nb_sem.at[n, 0])

        @pl.when(r < nr - 1)
        def _():
            arrived(nb_row.at[n, 1], nb_sem.at[n, 1])

        @pl.when(c > 0)
        def _():
            arrived(nb_col.at[n, 0], nb_sem.at[n, 2])

        @pl.when(c < nc - 1)
        def _():
            arrived(nb_col.at[n, 1], nb_sem.at[n, 3])

        @pl.when(is_row)
        def _():
            for slot in range(8):
                for i in range(k):
                    arrived(rx_row.at[n, slot, i], row_sem.at[n, slot, i])
            for i in range(k):
                nb_row[n, tr, i] = select(lambda s: rx_row[n, s, i], row_pick, length)

        @pl.when(is_col)
        def _():
            for slot in range(8):
                arrived(rx_col.at[n, slot], col_sem.at[n, slot])
            nb_col[n, tc] = select(lambda s: rx_col[n, s], col_pick, length)

    def gathered(n, end, b):
        lines = [nb_row[n, end, i, b * half_r : (b + 1) * half_r, :] for i in range(k)]
        if height > half_c:
            lines.append(jnp.zeros((height - half_c, LANES), jnp.float32))
        return jnp.concatenate(lines, axis=0)

    def from_left(x, line):
        return jnp.where(sub == 0, line, pltpu.roll(x, 1, 0))

    def from_right(x, line):
        return jnp.where(sub == half_c - 1, line, pltpu.roll(x, height - 1, 0))

    for end, y in ((0, 0), (1, rows - 1)):
        for i in range(k):
            for b in range(2):
                st_row[0, end, i, b * half_r : (b + 1) * half_r, :] = smoothed[y][b][
                    i * half_r : (i + 1) * half_r
                ]
    for y in range(rows):
        at = (y % 2) * half_r + y // 2
        st_col[0, 0, at : at + 1, :] = smoothed[y][0][0:1]
        st_col[0, 1, at : at + 1, :] = smoothed[y][1][half_c - 1 : half_c]
    pl.semaphore_wait(barrier, expected)
    start(0)

    def inner(y, b):
        x = smoothed[y][b]
        total = vertical[y][b] * upper(x) + low_vert[y][b] * lower(x) + smoothed[y][1 - b]
        if y > 0:
            total = total + smoothed[y - 1][b]
        if y < rows - 1:
            total = total + smoothed[y + 1][b]
        return total

    partial = fine(inner)

    def block_mean(values, i):
        y = 2 * i
        return 0.25 * (values[y][0] + values[y][1] + values[y + 1][0] + values[y + 1][1])

    small = range(half_r)
    c_vert = [block_mean(vertical, i) for i in small]
    c_low = [lower(c_vert[i]) for i in small]
    c_inv = [relaxation / (block_mean(gain, i) + 1.0 + c_vert[i] + c_low[i]) for i in small]

    receive(0, rows)

    def outer(y, b):
        at = (y % 2) * half_r + y // 2
        if b == 0:
            total = partial[y][b] + from_left(smoothed[y][1], nb_col[0, 0, at : at + 1, :])
        else:
            total = partial[y][b] + from_right(smoothed[y][0], nb_col[0, 1, at : at + 1, :])
        if y == 0:
            total = total + gathered(0, 0, b)
        if y == rows - 1:
            total = total + gathered(0, 1, b)
        return total

    off = fine(outer)
    residual = fine(lambda y, b: (1.0 - relaxation) * right_side[y][b] + off[y][b])
    guess = [c_inv[i] * block_mean(residual, i) for i in small]

    def stage_coarse(n, values):
        for end, i in ((0, 0), (1, half_r - 1)):
            for piece in range(k):
                st_row[n, end, piece, :half_r, :] = values[i][
                    piece * half_r : (piece + 1) * half_r
                ]
        for i in small:
            st_col[n, 0, i : i + 1, :] = values[i][0:1]
            st_col[n, 1, i : i + 1, :] = values[i][half_c - 1 : half_c]

    stage_coarse(1, guess)
    start(1)
    c_partial = []
    for i in small:
        x = guess[i]
        beside = jnp.zeros_like(x)
        if i > 0:
            beside = beside + guess[i - 1]
        if i < half_r - 1:
            beside = beside + guess[i + 1]
        c_partial.append(
            (beside, c_vert[i] * upper(x) + c_low[i] * lower(x))
        )
    receive(1, half_r)
    correction = []
    for i in small:
        beside, column = c_partial[i]
        beside = beside + from_left(guess[i], nb_col[1, 0, i : i + 1, :])
        beside = beside + from_right(guess[i], nb_col[1, 1, i : i + 1, :])
        if i == 0:
            beside = beside + gathered(1, 0, 0)
        if i == half_r - 1:
            beside = beside + gathered(1, 1, 0)
        correction.append(
            (2.0 - relaxation) * guess[i] + c_inv[i] * (0.25 * beside + column)
        )

    stage_coarse(2, correction)
    start(2)
    c_up = [upper(x) for x in correction]
    c_down = [lower(x) for x in correction]

    def base(y, b):
        i = y // 2
        total = off[y][b] + 2.0 * correction[i]
        total = total + vertical[y][b] * c_up[i] + low_vert[y][b] * c_down[i]
        other = i - 1 if y % 2 == 0 else i + 1
        if 0 <= other < half_r:
            total = total + correction[other]
        return (
            (2.0 - relaxation) * smoothed[y][b] + (1.0 - relaxation) * correction[i],
            total,
        )

    bases = fine(base)
    for i in small:
        small_ref[i] = correction[i]
    receive(2, half_r)
    left = [from_left(correction[i], nb_col[2, 0, i : i + 1, :]) for i in small]
    right = [from_right(correction[i], nb_col[2, 1, i : i + 1, :]) for i in small]
    top = gathered(2, 0, 0)
    bottom = gathered(2, 1, 0)
    for y, b in every:
        first, total = bases[y][b]
        total = total + (left if b == 0 else right)[y // 2]
        if y == 0:
            total = total + top
        if y == rows - 1:
            total = total + bottom
        spread[y, pl.ds(b, height, stride=2), :] = first + inverse[y][b] * total
    for n in range(3):
        finish_sends(n)


def unpack(spread, small_ref, sol_ref, corr_ref):
    panels, _, cols, levels = sol_ref.shape
    half_c = corr_ref.shape[2]
    for p in range(panels):
        lanes = slice(p * levels, (p + 1) * levels)
        sol_ref[p] = spread[:, :cols, lanes]
        corr_ref[p] = small_ref[:, :half_c, lanes]


def solution(mesh):
    nr, nc = mesh.shape["tx"], mesh.shape["ty"]

    def shards(residual, density, gain, vertical, edge_panel, edge_side, edge_flip):
        panels, rows, cols, levels = residual.shape
        k = cols // rows
        assert cols == k * rows and rows % 2 == 0 and panels * levels <= LANES
        seg_h = round_up(rows, 8)
        height = round_up(cols // 2, 8)
        tall = 2 * height
        f32 = jnp.float32
        spread, small = pl.pallas_call(
            functools.partial(kernel, nr, nc),
            out_shape=(
                jax.ShapeDtypeStruct((rows, tall, LANES), f32),
                jax.ShapeDtypeStruct((rows // 2, height, LANES), f32),
            ),
            in_specs=[pl.BlockSpec(memory_space=pl.ANY)] * 4
            + [pl.BlockSpec(memory_space=pltpu.SMEM)] * 3,
            out_specs=(pl.BlockSpec(memory_space=pltpu.VMEM),) * 2,
            scratch_shapes=[
                pltpu.VMEM((4, panels, rows, cols, levels), f32),
                pltpu.VMEM((3, rows, tall, LANES), f32),
                pltpu.VMEM((4, 2, k, seg_h, LANES), f32),
                pltpu.VMEM((4, 2, seg_h, LANES), f32),
                pltpu.VMEM((4, 2, k, seg_h, LANES), f32),
                pltpu.VMEM((4, 2, seg_h, LANES), f32),
                pltpu.VMEM((3, 8, k, seg_h, LANES), f32),
                pltpu.VMEM((3, 8, seg_h, LANES), f32),
                pltpu.SemaphoreType.DMA((4,)),
                pltpu.SemaphoreType.DMA((3, 4 + 8 * k + 4 + 4)),
                pltpu.SemaphoreType.DMA((3, 4)),
                pltpu.SemaphoreType.DMA((3, 8, k)),
                pltpu.SemaphoreType.DMA((3, 8)),
            ],
            compiler_params=pltpu.CompilerParams(collective_id=0, has_side_effects=True),
        )(residual, density, gain, vertical, edge_panel.T, edge_side.T, edge_flip.T)
        return pl.pallas_call(
            unpack,
            out_shape=(
                jax.ShapeDtypeStruct(residual.shape, f32),
                jax.ShapeDtypeStruct((panels, rows // 2, cols // 2, levels), f32),
            ),
            in_specs=[pl.BlockSpec(memory_space=pltpu.VMEM)] * 2,
            out_specs=(pl.BlockSpec(memory_space=pltpu.VMEM),) * 2,
        )(spread, small)

    fields = P(None, "tx", "ty", None)
    return jax.shard_map(
        shards,
        mesh=mesh,
        in_specs=(fields,) * 4 + (P(),) * 3,
        out_specs=(fields, fields),
        check_vma=False,
    )
```

profile of v0, /device:TPU:0, one launch (start us, length us, event | category | flops | bytes accessed | tf_op | source)
XLA Modules:
  0.0 25.3 jit_solution(17043933451593448772)
XLA Ops:
  0.6 23.0 %shard_map.86 = (f32[6,16,128]{2,1,0:T(8,128)}, f32[3,8,128]{2,1,0:T(8,128)}) custom-call(f32[6,6,12,16]{3,2,1,0:T(8,128)} %res_hbm.1, f32[6,6,12,16]{3,2,1,0:T(8,128)} %den_hbm.1, f32[6,6,12,16]{3,2,1,0:T(8,128)} %gain_hbm.1, f32[6,6,12,16]{3,2,1,0:T(8,128)} %vert_hbm.1, s32[4,6]{1,0:T(4,128)} %bitcast.3, s32[4,6]{1,0:T(4,128)} %bitcast.4, s32[4,6]{1,0:T(4,128)} %bitcast.5), custom_call_target="tpu_custom_call" | custom-call | tf_op jit(solution)/shard_map/pallas_call | solution.py:424
  23.7 1.7 %shard_map.87 = (f32[6,6,12,16]{3,2,1,0:T(8,128)}, f32[6,3,6,16]{3,2,1,0:T(8,128)}) custom-call(f32[6,16,128]{2,1,0:T(8,128)} %get-tuple-element.4.spread, f32[3,8,128]{2,1,0:T(8,128)} %get-tuple-element.5.small_ref), custom_call_target="tpu_custom_call" | custom-call | tf_op jit(solution)/shard_map/pallas_call | solution.py:450
where the time goes:
time: 25.6 us; the launch traced here: 25.3 us
  Pallas kernels  24.7 us (96%)
  between operations  0.64 us (2%)
    pallas_call x1, Pallas kernels, shards(): pl.pallas_call(functools.partial(kernel, nr, nc), out_shape=(jax.ShapeDty...  23 us
    pallas_call x1, Pallas kernels, shards(): pl.pallas_call(unpack, out_shape=(jax.ShapeDtypeStruct(residual.shape, f3...  1.67 us

commit v1 on v0

v1 whole, which is shorter than its diff:
```python
import functools

import jax
import jax.numpy as jnp
from jax import lax
from jax.experimental import pallas as pl
from jax.experimental.pallas import tpu as pltpu
from jax.sharding import PartitionSpec as P

MESH = pl.DeviceIdType.MESH
relaxation = 0.8
LANES = 128
TILE = 8


def round_up(value, unit):
    return (value + unit - 1) // unit * unit


def kernel(
    nr,
    nc,
    res_hbm,
    den_hbm,
    gain_hbm,
    vert_hbm,
    panel_ref,
    side_ref,
    flip_ref,
    spread,
    small_ref,
    inp,
    packed,
    st_row,
    st_col,
    ex_row,
    ex_col,
    nb_row,
    nb_col,
    corner,
    rx_row,
    rx_col,
    ry_row,
    ry_col,
    in_sem,
    send_sem,
    nb_sem,
    corner_sem,
    row_sem,
    col_sem,
    row_end_sem,
    col_end_sem,
):
    _, panels, rows, cols, levels = inp.shape
    half_r, half_c = rows // 2, cols // 2
    k = cols // rows
    length = half_r
    last = length - 1
    height = spread.shape[1] // 2
    block = st_row.shape[3]
    r = lax.axis_index("tx")
    c = lax.axis_index("ty")
    is_row = (r == 0) | (r == nr - 1)
    is_col = (c == 0) | (c == nc - 1)
    tr = r // (nr - 1)
    tc = c // (nc - 1)
    row_ok = (r > 0, r < nr - 1)
    col_ok = (c > 0, c < nc - 1)

    def row_segment(f, p):
        return k * c + p if f == 0 else nr - 1 - k * c - p

    def col_segment(f):
        return r if f == 0 else nr - 1 - r

    def clamp(x, n):
        return jnp.minimum(jnp.maximum(x, 0), n - 1)

    def partners():
        found = []
        for f in range(2):
            here = c if f == 0 else nc - 1 - c
            for e in range(2):
                for d in (-1, 0, 1):
                    to = here + d
                    found.append((is_row & (to >= 0) & (to < nc), (e * (nr - 1), clamp(to, nc))))
                low = row_segment(f, 0 if f == 0 else k - 1)
                for d in range(-1, k + 1):
                    to = low + d
                    found.append((is_row & (to >= 0) & (to < nr), (clamp(to, nr), e * (nc - 1))))
                g = col_segment(f)
                for d in (-1, 0, 1):
                    to = g + d
                    inside = is_col & (to >= 0) & (to < nr)
                    found.append((inside, (clamp(to, nr), e * (nc - 1))))
                    if d:
                        inside = inside & (g % k == (k - 1 if d == 1 else 0))
                    found.append((inside, (e * (nr - 1), clamp(g // k + d, nc))))
        for dr in (-1, 0, 1):
            for dc in (-1, 0, 1):
                if dr or dc:
                    ok = True
                    if dr:
                        ok = row_ok[(dr + 1) // 2]
                    if dc:
                        ok = col_ok[(dc + 1) // 2] if ok is True else ok & col_ok[(dc + 1) // 2]
                    found.append((ok, (r + dr, c + dc)))
        return found

    def messages():
        found = []
        src_row = st_row.at[tr]
        for f in range(2):
            slot = 4 * f + tr
            to = c if f == 0 else nc - 1 - c
            for e in range(2):
                found.append((is_row, (e * (nr - 1), to), src_row, rx_row.at[slot], row_sem))
        for f in range(2):
            slot = 4 * f + 2 + tc
            g = col_segment(f)
            for e in range(2):
                found.append(
                    (is_col, (g, e * (nc - 1)), st_col.at[tc], rx_col.at[slot], col_sem)
                )
                found.append(
                    (
                        is_col,
                        (e * (nr - 1), g // k),
                        st_col.at[tc],
                        rx_row.at[slot, r % k],
                        row_sem,
                    )
                )
        for p in range(k):
            for f in range(2):
                slot = 4 * f + tr
                g = row_segment(f, p)
                for e in range(2):
                    found.append(
                        (is_row, (g, e * (nc - 1)), st_row.at[tr, p], rx_col.at[slot], col_sem)
                    )
        for h in range(2):
            for f in range(2):
                d = 1 if h != f else -1
                end = 0 if d == 1 else 1
                for p in range(k):
                    slot = 4 * f + tr
                    src = ex_row.at[tr, p, h]
                    to = row_segment(f, p) + d
                    ok = is_row & (to >= 0) & (to < nr)
                    for e in range(2):
                        found.append(
                            (
                                ok,
                                (clamp(to, nr), e * (nc - 1)),
                                src,
                                ry_col.at[end, slot],
                                col_end_sem.at[end],
                            )
                        )
                    if p == (k - 1 if h == 1 else 0):
                        to = (c if f == 0 else nc - 1 - c) + d
                        ok = is_row & (to >= 0) & (to < nc)
                        for e in range(2):
                            found.append(
                                (
                                    ok,
                                    (e * (nr - 1), clamp(to, nc)),
                                    src,
                                    ry_row.at[end, slot],
                                    row_end_sem.at[end],
                                )
                            )
                slot = 4 * f + 2 + tc
                src = ex_col.at[tc, h]
                g = col_segment(f)
                to = g + d
                ok = is_col & (to >= 0) & (to < nr)
                far = ok & (g % k == (k - 1 if d == 1 else 0))
                for e in range(2):
                    found.append(
                        (ok, (clamp(to, nr), e * (nc - 1)), src, ry_col.at[end, slot], col_end_sem.at[end])
                    )
                    found.append(
                        (
                            far,
                            (e * (nr - 1), clamp(g // k + d, nc)),
                            src,
                            ry_row.at[end, slot],
                            row_end_sem.at[end],
                        )
                    )
        border = len(found)
        for s in range(2):
            found.append(
                (row_ok[s], (r + 2 * s - 1, c), st_row.at[s], nb_row.at[1 - s], nb_sem.at[1 - s])
            )
            found.append(
                (
                    col_ok[s],
                    (r, c + 2 * s - 1),
                    st_col.at[s],
                    nb_col.at[1 - s],
                    nb_sem.at[3 - s],
                )
            )
        for s in range(2):
            for w in range(2):
                at = 2 * (1 - s) + 1 - w
                found.append(
                    (
                        row_ok[s] & col_ok[w],
                        (r + 2 * s - 1, c + 2 * w - 1),
                        ex_row.at[s, w * (k - 1), w],
                        corner.at[at],
                        corner_sem.at[at],
                    )
                )
        return found, border

    def same(dest):
        return (dest[0] == r) & (dest[1] == c)

    loads = [
        pltpu.make_async_copy(source, inp.at[i], in_sem.at[i])
        for i, source in enumerate((gain_hbm, vert_hbm, den_hbm, res_hbm))
    ]
    for load in loads:
        load.start()

    barrier = pltpu.get_barrier_semaphore()
    expected = jnp.int32(0)
    for active, dest in partners():
        go = active & jnp.logical_not(same(dest))
        expected = expected + go.astype(jnp.int32)

        @pl.when(go)
        def _():
            pl.semaphore_signal(barrier, inc=1, device_id=dest, device_id_type=MESH)

    lane = lax.broadcasted_iota(jnp.int32, (TILE, LANES), 1)
    sub = lax.broadcasted_iota(jnp.int32, (height, LANES), 0)
    level = lane[:1] % levels
    first_level = level == 0
    last_level = level == levels - 1

    def lower(x):
        return jnp.where(first_level, 0.0, pltpu.roll(x, 1, 1))

    def upper(x):
        return jnp.where(last_level, 0.0, pltpu.roll(x, LANES - 1, 1))

    def pick_tables(side):
        index = lane
        code = jnp.zeros_like(lane)
        for p in range(panels):
            here = lane // levels == p
            index = jnp.where(here, panel_ref[side, p] * levels + lane % levels, index)
            code = jnp.where(here, flip_ref[side, p] * 4 + side_ref[side, p], code)
        return index, code

    row_pick = pick_tables(tr)
    col_pick = pick_tables(2 + tc)

    def pack(value):
        filler = jnp.zeros((rows, cols, LANES - panels * levels), jnp.float32)
        return jnp.concatenate([value[p] for p in range(panels)] + [filler], axis=-1)

    def split(which, value):
        packed[which, :, :cols, :] = value
        if packed.shape[2] > cols:
            packed[which, :, cols:, :] = jnp.zeros(
                (rows, packed.shape[2] - cols, LANES), jnp.float32
            )
        return [
            [packed[which, y, pl.ds(b, height, stride=2), :] for b in range(2)]
            for y in range(rows)
        ]

    def fine(fun):
        return [[fun(y, b) for b in range(2)] for y in range(rows)]

    small = range(half_r)

    def block_mean(values, i):
        y = 2 * i
        return 0.25 * (values[y][0] + values[y][1] + values[y + 1][0] + values[y + 1][1])

    loads[0].wait()
    gain = split(1, pack(inp[0]))
    loads[1].wait()
    vertical = split(2, pack(inp[1]))
    low_vert = fine(lambda y, b: lower(vertical[y][b]))
    inverse = fine(
        lambda y, b: relaxation / (gain[y][b] + 4.0 + vertical[y][b] + low_vert[y][b])
    )
    c_vert = [block_mean(vertical, i) for i in small]
    c_low = [lower(c_vert[i]) for i in small]
    c_inv = [relaxation / (block_mean(gain, i) + 1.0 + c_vert[i] + c_low[i]) for i in small]
    loads[2].wait()
    loads[3].wait()
    right_side = split(0, pack(inp[2] * inp[3]))
    smoothed = fine(lambda y, b: inverse[y][b] * right_side[y][b])

    def inner(y, b):
        x = smoothed[y][b]
        return vertical[y][b] * upper(x) + low_vert[y][b] * lower(x)

    coupled = fine(inner)
    column = fine(lambda y, b: coupled[y][b] + (1.0 - relaxation) * right_side[y][b])
    north = [smoothed[2 * i][0] + smoothed[2 * i][1] for i in small]
    south = [smoothed[2 * i + 1][0] + smoothed[2 * i + 1][1] for i in small]
    west = [smoothed[2 * i][0] + smoothed[2 * i + 1][0] for i in small]
    east = [smoothed[2 * i][1] + smoothed[2 * i + 1][1] for i in small]
    from_w = [pltpu.roll(east[i], 1, 0) for i in small]
    from_e = [pltpu.roll(west[i], height - 1, 0) for i in small]
    start_w = sub % length == 0
    start_e = sub % length == last
    edge_w = sub == 0
    edge_e = sub == half_c - 1

    def bare(i):
        total = block_mean(column, i) + 0.5 * (north[i] + south[i])
        beside = None
        if i > 0:
            beside = south[i - 1]
        if i < half_r - 1:
            beside = north[i + 1] if beside is None else beside + north[i + 1]
        return total if beside is None else total + 0.25 * beside

    plain = [bare(i) for i in small]

    def partial_guess(i, mask_w, mask_e):
        beside = jnp.where(mask_w, 0.0, from_w[i]) + jnp.where(mask_e, 0.0, from_e[i])
        return c_inv[i] * (plain[i] + 0.25 * beside)

    by_tile = [partial_guess(i, edge_w, edge_e) for i in small]
    by_piece = by_tile if k == 1 else [partial_guess(i, start_w, start_e) for i in small]

    def put(ref, at, value):
        ref[at : at + value.shape[0], :] = value

    for s in range(2):
        y = s * (rows - 1)
        i0, i1 = (0, 1) if s == 0 else (half_r - 1, half_r - 2)
        out = north[0] if s == 0 else south[half_r - 1]
        for p in range(k):
            lo, hi = p * length, p * length + last
            seg = slice(lo, hi + 1)
            one = lambda x, j: x[j : j + 1]
            a, b, g = (st_row.at[s, p, q] for q in range(3))
            put(a, 0, smoothed[y][0][seg])
            put(a, length, smoothed[y][1][seg])
            put(a, 2 * length, one(c_inv[i1], lo))
            put(a, 2 * length + 1, one(c_inv[i1], hi))
            put(b, 0, by_piece[i0][seg])
            put(b, length, by_piece[i1][seg])
            put(b, 2 * length, one(west[i0], lo))
            put(b, 2 * length + 1, one(east[i0], hi))
            put(g, 0, c_inv[i0][seg])
            put(g, length, c_vert[i0][seg])
            put(g, 2 * length, one(west[i1], lo))
            put(g, 2 * length + 1, one(east[i1], hi))
            for h in range(2):
                j, j1 = (lo, lo + 1) if h == 0 else (hi, hi - 1)
                side = west if h == 0 else east
                x = ex_row.at[s, p, h]
                put(x, 0, one(by_piece[i0], j))
                put(x, 1, one(c_inv[i0], j))
                put(x, 2, one(side[i0], j))
                put(x, 3, one(side[i1], j))
                put(x, 4, one(out, j))
                put(x, 5, one(out, j1))
    for s in range(2):
        j0, j1 = (0, 1) if s == 0 else (half_c - 1, half_c - 2)
        out = west if s == 0 else east
        a, b, g = (st_col.at[s, q] for q in range(3))
        at0 = lambda x: x[j0 : j0 + 1]
        at1 = lambda x: x[j1 : j1 + 1]
        for y in range(rows):
            put(a, (y % 2) * length + y // 2, at0(smoothed[y][s]))
        put(a, 2 * length, at1(c_inv[0]))
        put(a, 2 * length + 1, at1(c_inv[half_r - 1]))
        for i in small:
            put(b, i, at0(by_tile[i]))
            put(b, length + i, at1(by_tile[i]))
            put(g, i, at0(c_inv[i]))
            put(g, length + i, at0(c_vert[i]))
        put(b, 2 * length, at0(north[0]))
        put(b, 2 * length + 1, at0(south[half_r - 1]))
        put(g, 2 * length, at1(north[0]))
        put(g, 2 * length + 1, at1(south[half_r - 1]))
        for h in range(2):
            i0, i1 = (0, 1) if h == 0 else (half_r - 1, half_r - 2)
            side = north[0] if h == 0 else south[half_r - 1]
            x = ex_col.at[s, h]
            put(x, 0, at0(by_tile[i0]))
            put(x, 1, at0(c_inv[i0]))
            put(x, 2, at0(side))
            put(x, 3, at1(side))
            put(x, 4, at0(out[i0]))
            put(x, 5, at0(out[i1]))

    sends, border = messages()
    pl.semaphore_wait(barrier, expected)
    for m, (active, dest, src, dst, sem) in enumerate(sends):
        mine = same(dest)

        @pl.when(active & jnp.logical_not(mine) if m < border else active)
        def _():
            pltpu.make_async_remote_copy(
                src_ref=src,
                dst_ref=dst,
                send_sem=send_sem.at[m],
                recv_sem=sem,
                device_id=dest,
                device_id_type=MESH,
            ).start()

        if m < border:

            @pl.when(active & mine)
            def _():
                pltpu.make_async_copy(src, dst, sem).start()

    def beside(y, b):
        x = smoothed[y][b]
        total = coupled[y][b] + smoothed[y][1 - b]
        if y > 0:
            total = total + smoothed[y - 1][b]
        if y < rows - 1:
            total = total + smoothed[y + 1][b]
        return total

    partial = fine(beside)

    def arrived(ref, sem):
        pltpu.make_async_copy(ref, ref, sem).wait()

    for s in range(2):

        @pl.when(row_ok[s])
        def _():
            arrived(nb_row.at[s], nb_sem.at[s])

        @pl.when(col_ok[s])
        def _():
            arrived(nb_col.at[s], nb_sem.at[2 + s])

        for w in range(2):

            @pl.when(row_ok[s] & col_ok[w])
            def _():
                arrived(corner.at[2 * s + w], corner_sem.at[2 * s + w])

    order = list(range(2 * length))[::-1] + [2 * length + 1, 2 * length]
    other = (
        list(range(length))[::-1]
        + list(range(length, 2 * length))[::-1]
        + [2 * length + 1, 2 * length]
    )
    sublane = lax.broadcasted_iota(jnp.int32, (block, LANES), 0)

    def flip_index(perm):
        index = sublane
        for at, source in enumerate(perm):
            index = jnp.where(sublane == at, source, index)
        return index

    flips = [flip_index(order), flip_index(other), flip_index(other)]

    def choose(read, pick, f):
        index, code = pick
        taken = None
        for t in range(4):
            moved = jnp.take_along_axis(read(4 * f + t), index, axis=1, mode="promise_in_bounds")
            taken = moved if taken is None else jnp.where(code == 4 * f + t, moved, taken)
        return taken

    def select(plainly, reverse, pick, group):
        straight = choose(plainly, pick, 0)
        turned = choose(reverse, pick, 1)
        if group is not None:
            turned = jnp.take_along_axis(turned, flips[group], axis=0, mode="promise_in_bounds")
        return jnp.where(pick[1] >= 4, turned, straight)

    @pl.when(is_row)
    def _():
        arrived(rx_row, row_sem)
        for p in range(k):
            for q in range(3):
                nb_row[tr, p, q] = select(
                    lambda s: rx_row[s, p, q], lambda s: rx_row[s, k - 1 - p, q], row_pick, q
                )
        for w in range(2):

            @pl.when(col_ok[w])
            def _():
                arrived(ry_row.at[w], row_end_sem.at[w])
                read = lambda s: ry_row[w, s]
                corner[2 * tr + w] = select(read, read, row_pick, None)

    @pl.when(is_col)
    def _():
        arrived(rx_col, col_sem)
        for q in range(3):
            read = lambda s: rx_col[s, q]
            nb_col[tc, q] = select(read, read, col_pick, q)
        for s in range(2):

            @pl.when(row_ok[s])
            def _():
                arrived(ry_col.at[s], col_end_sem.at[s])
                read = lambda slot: ry_col[s, slot]
                value = select(read, read, col_pick, None)
                corner[2 * s + tc, 0:2, :] = value[0:2]
                corner[2 * s + tc, 2:4, :] = value[4:6]
                corner[2 * s + tc, 4:6, :] = value[2:4]

    @pl.when(is_row & is_col)
    def _():
        at = 2 * tr + tc
        corner[at, 0:2, :] = jnp.zeros((2, LANES), jnp.float32)
        for q in range(2):
            rows_z = nb_col[tc, 1 + q]
            rows_x = nb_row[tr, tc * (k - 1), 1 + q]
            corner[at, 2 + q : 3 + q, :] = jnp.where(
                tr == 0, rows_z[2 * length : 2 * length + 1], rows_z[2 * length + 1 : 2 * length + 2]
            )
            corner[at, 4 + q : 5 + q, :] = jnp.where(
                tc == 0, rows_x[2 * length : 2 * length + 1], rows_x[2 * length + 1 : 2 * length + 2]
            )

    def zeros(count):
        return [jnp.zeros((count, LANES), jnp.float32)] if count else []

    def stack(lines, total):
        used = sum(x.shape[0] for x in lines)
        return jnp.concatenate(list(lines) + zeros(total - used), axis=0)

    tall_z = round_up(half_r, TILE)
    flat = 2 * length

    class Strip:
        pass

    def strip(read, pieces, ends, total, own):
        def gather(q, at):
            return stack([read(p, q, slice(at, at + length)) for p in range(pieces)], total)

        def sides(first, final):
            lines = []
            for p in range(pieces):
                lines += [first(p)] + zeros(length - 2) + [final(p)]
            return stack(lines, total)

        def lateral(q):
            return sides(
                lambda p: ends[0][q] if p == 0 else read(p - 1, 1 + q, slice(flat + 1, flat + 2)),
                lambda p: ends[1][q]
                if p == pieces - 1
                else read(p + 1, 1 + q, slice(flat, flat + 1)),
            )

        x = Strip()
        x.even, x.odd = gather(0, 0), gather(0, length)
        x.pair = x.even + x.odd
        inv1 = sides(
            lambda p: read(p, 0, slice(flat, flat + 1)),
            lambda p: read(p, 0, slice(flat + 1, flat + 2)),
        )
        x.inv, x.vert = gather(2, 0), gather(2, length)
        x.guess = gather(1, 0) + 0.25 * x.inv * (lateral(0) + own)
        x.inside = gather(1, length) + 0.25 * inv1 * lateral(1)
        return x

    def corner_row(s, w, at):
        return corner[2 * s + w, at : at + 1, :]

    row_strip = []
    for s in range(2):
        own = north[0] if s == 0 else south[half_r - 1]
        ends = [[corner_row(s, w, 2 + q) for q in range(2)] for w in range(2)]
        row_strip.append(
            strip(lambda p, q, rows_: nb_row[s, p, q, rows_, :], k, ends, height, own)
        )
    col_strip = []
    for w in range(2):
        j = w * (half_c - 1)
        faces = west if w == 0 else east
        own = stack([faces[i][j : j + 1] for i in small], tall_z)
        ends = [[corner_row(s, w, 4 + q) for q in range(2)] for s in range(2)]
        col_strip.append(
            strip(lambda p, q, rows_: nb_col[w, q, rows_, :], 1, ends, tall_z, own)
        )

    guess = []
    for i in small:
        lateral = jnp.where(edge_w, col_strip[0].pair[i : i + 1], 0.0)
        lateral = lateral + jnp.where(edge_e, col_strip[1].pair[i : i + 1], 0.0)
        if i == 0:
            lateral = lateral + row_strip[0].pair
        if i == half_r - 1:
            lateral = lateral + row_strip[1].pair
        guess.append(by_tile[i] + 0.25 * c_inv[i] * lateral)

    row_side = [[None] * 2 for _ in range(2)]
    col_side = [[None] * 2 for _ in range(2)]
    for s in range(2):
        for w in range(2):
            faces = nb_row[s, w * (k - 1), 1, flat + w : flat + w + 1, :]
            faces = faces + nb_col[w, 1, flat + s : flat + s + 1, :]
            there = corner_row(s, w, 0) + 0.25 * corner_row(s, w, 1) * faces
            tip = (r == s * (nr - 1)) & (c == w * (nc - 1))
            jr, jc = w * (half_c - 1), s * (half_r - 1)
            row_side[s][w] = jnp.where(tip, col_strip[w].guess[jc : jc + 1], there)
            col_side[w][s] = jnp.where(tip, row_strip[s].guess[jr : jr + 1], there)

    def relax(x, ends, own, count):
        total = x.guess.shape[0]
        at = lax.broadcasted_iota(jnp.int32, (total, LANES), 0)
        around = x.inside + own
        around = around + jnp.where(at == 0, ends[0], pltpu.roll(x.guess, 1, 0))
        around = around + jnp.where(at == count - 1, ends[1], pltpu.roll(x.guess, total - 1, 0))
        column = x.vert * upper(x.guess) + lower(x.vert) * lower(x.guess)
        return (2.0 - relaxation) * x.guess + x.inv * (0.25 * around + column)

    row_fix = [
        relax(row_strip[s], row_side[s], guess[s * (half_r - 1)], half_c) for s in range(2)
    ]
    col_fix = []
    for w in range(2):
        j = w * (half_c - 1)
        own = stack([guess[i][j : j + 1] for i in small], tall_z)
        col_fix.append(relax(col_strip[w], col_side[w], own, half_r))

    def from_left(x, line):
        return jnp.where(edge_w, line, pltpu.roll(x, 1, 0))

    def from_right(x, line):
        return jnp.where(edge_e, line, pltpu.roll(x, height - 1, 0))

    correction = []
    for i in small:
        x = guess[i]
        around = from_left(x, col_strip[0].guess[i : i + 1])
        around = around + from_right(x, col_strip[1].guess[i : i + 1])
        around = around + (guess[i - 1] if i > 0 else row_strip[0].guess)
        around = around + (guess[i + 1] if i < half_r - 1 else row_strip[1].guess)
        levels_part = c_vert[i] * upper(x) + c_low[i] * lower(x)
        correction.append((2.0 - relaxation) * x + c_inv[i] * (0.25 * around + levels_part))
        small_ref[i] = correction[i]

    def outer(y, b):
        at = (y % 2) * length + y // 2
        source = col_strip[b]
        line = (source.even if y % 2 == 0 else source.odd)[y // 2 : y // 2 + 1]
        if b == 0:
            total = partial[y][b] + from_left(smoothed[y][1], line)
        else:
            total = partial[y][b] + from_right(smoothed[y][0], line)
        if y == 0:
            total = total + (row_strip[0].even if b == 0 else row_strip[0].odd)
        if y == rows - 1:
            total = total + (row_strip[1].even if b == 0 else row_strip[1].odd)
        return total

    c_up = [upper(x) for x in correction]
    c_down = [lower(x) for x in correction]
    left = [from_left(correction[i], col_fix[0][i : i + 1]) for i in small]
    right = [from_right(correction[i], col_fix[1][i : i + 1]) for i in small]
    for y in range(rows):
        i = y // 2
        next_i = i - 1 if y % 2 == 0 else i + 1
        for b in range(2):
            total = outer(y, b) + 2.0 * correction[i]
            total = total + vertical[y][b] * c_up[i] + low_vert[y][b] * c_down[i]
            if next_i < 0:
                total = total + row_fix[0]
            elif next_i >= half_r:
                total = total + row_fix[1]
            else:
                total = total + correction[next_i]
            total = total + (left if b == 0 else right)[i]
            first = (2.0 - relaxation) * smoothed[y][b] + (1.0 - relaxation) * correction[i]
            spread[y, pl.ds(b, height, stride=2), :] = first + inverse[y][b] * total

    for m, (active, dest, src, dst, sem) in enumerate(sends):

        @pl.when(active & jnp.logical_not(same(dest)) if m < border else active)
        def _():
            pltpu.make_async_copy(src, src, send_sem.at[m]).wait()


def unpack(spread, small_ref, sol_ref, corr_ref):
    panels, _, cols, levels = sol_ref.shape
    half_c = corr_ref.shape[2]
    for p in range(panels):
        lanes = slice(p * levels, (p + 1) * levels)
        sol_ref[p] = spread[:, :cols, lanes]
        corr_ref[p] = small_ref[:, :half_c, lanes]


def solution(mesh):
    nr, nc = mesh.shape["tx"], mesh.shape["ty"]

    def shards(residual, density, gain, vertical, edge_panel, edge_side, edge_flip):
        panels, rows, cols, levels = residual.shape
        k = cols // rows
        assert cols == k * rows and rows % 2 == 0 and panels * levels <= LANES
        assert rows >= 6 and nr > 1 and nc > 1
        block = round_up(rows + 2, TILE)
        height = round_up(cols // 2, TILE)
        tall = 2 * height
        f32 = jnp.float32
        count = 4 + 8 + 4 * k + 8 * k + 8 + 16 + 4 + 4
        spread, small = pl.pallas_call(
            functools.partial(kernel, nr, nc),
            out_shape=(
                jax.ShapeDtypeStruct((rows, tall, LANES), f32),
                jax.ShapeDtypeStruct((rows // 2, height, LANES), f32),
            ),
            in_specs=[pl.BlockSpec(memory_space=pl.ANY)] * 4
            + [pl.BlockSpec(memory_space=pltpu.SMEM)] * 3,
            out_specs=(pl.BlockSpec(memory_space=pltpu.VMEM),) * 2,
            scratch_shapes=[
                pltpu.VMEM((4, panels, rows, cols, levels), f32),
                pltpu.VMEM((3, rows, tall, LANES), f32),
                pltpu.VMEM((3, k, 3, block, LANES), f32),
                pltpu.VMEM((3, 3, block, LANES), f32),
                pltpu.VMEM((3, k, 2, TILE, LANES), f32),
                pltpu.VMEM((3, 2, TILE, LANES), f32),
                pltpu.VMEM((3, k, 3, block, LANES), f32),
                pltpu.VMEM((3, 3, block, LANES), f32),
                pltpu.VMEM((5, TILE, LANES), f32),
                pltpu.VMEM((8, k, 3, block, LANES), f32),
                pltpu.VMEM((8, 3, block, LANES), f32),
                pltpu.VMEM((2, 8, TILE, LANES), f32),
                pltpu.VMEM((2, 8, TILE, LANES), f32),
                pltpu.SemaphoreType.DMA((4,)),
                pltpu.SemaphoreType.DMA((count,)),
                pltpu.SemaphoreType.DMA((4,)),
                pltpu.SemaphoreType.DMA((4,)),
                pltpu.SemaphoreType.DMA,
                pltpu.SemaphoreType.DMA,
                pltpu.SemaphoreType.DMA((2,)),
                pltpu.SemaphoreType.DMA((2,)),
            ],
            compiler_params=pltpu.CompilerParams(collective_id=0, has_side_effects=True),
        )(residual, density, gain, vertical, edge_panel.T, edge_side.T, edge_flip.T)
        return pl.pallas_call(
            unpack,
            out_shape=(
                jax.ShapeDtypeStruct(residual.shape, f32),
                jax.ShapeDtypeStruct((panels, rows // 2, cols // 2, levels), f32),
            ),
            in_specs=[pl.BlockSpec(memory_space=pltpu.VMEM)] * 2,
            out_specs=(pl.BlockSpec(memory_space=pltpu.VMEM),) * 2,
        )(spread, small)

    fields = P(None, "tx", "ty", None)
    return jax.shard_map(
        shards,
        mesh=mesh,
        in_specs=(fields,) * 4 + (P(),) * 3,
        out_specs=(fields, fields),
        check_vma=False,
    )
```

time: 25.6 us -> 19.1 us (0.75)
  Pallas kernels: 24.7 us -> 18.3 us
    pallas_call x1, Pallas kernels: 23 us -> 16.6 us  [shards(): pl.pallas_call(functools.partial(kernel, nr, nc), out_shape=(jax.ShapeDty...]
where the time goes in v1:
time: 19.1 us; the launch traced here: 18.9 us
  Pallas kernels  18.3 us (96%)
  between operations  0.64 us (3%)
    pallas_call x1, Pallas kernels, shards(): pl.pallas_call(functools.partial(kernel, nr, nc), out_shape=(jax.ShapeDty...  16.6 us
    pallas_call x1, Pallas kernels, shards(): pl.pallas_call(unpack, out_shape=(jax.ShapeDtypeStruct(residual.shape, f3...  1.67 us

profile of v1, /device:TPU:0, one launch (start us, length us, event | category | flops | bytes accessed | tf_op | source)
XLA Modules:
  0.0 18.9 jit_solution(5978518223047826833)
XLA Ops:
  0.6 16.6 %shard_map.86 = (f32[6,16,128]{2,1,0:T(8,128)}, f32[3,8,128]{2,1,0:T(8,128)}) custom-call(f32[6,6,12,16]{3,2,1,0:T(8,128)} %res_hbm.1, f32[6,6,12,16]{3,2,1,0:T(8,128)} %den_hbm.1, f32[6,6,12,16]{3,2,1,0:T(8,128)} %gain_hbm.1, f32[6,6,12,16]{3,2,1,0:T(8,128)} %vert_hbm.1, s32[4,6]{1,0:T(4,128)} %bitcast.3, s32[4,6]{1,0:T(4,128)} %bitcast.4, s32[4,6]{1,0:T(4,128)} %bitcast.5), custom_call_target="tpu_custom_call" | custom-call | tf_op jit(solution)/shard_map/pallas_call | solution.py:717
  17.3 1.7 %shard_map.87 = (f32[6,6,12,16]{3,2,1,0:T(8,128)}, f32[6,3,6,16]{3,2,1,0:T(8,128)}) custom-call(f32[6,16,128]{2,1,0:T(8,128)} %get-tuple-element.4.spread, f32[3,8,128]{2,1,0:T(8,128)} %get-tuple-element.5.small_ref), custom_call_target="tpu_custom_call" | custom-call | tf_op jit(solution)/shard_map/pallas_call | solution.py:751

commit v2 on v1

--- a/solution.py
+++ b/solution.py
@@ -24,12 +24,13 @@
     den_hbm,
     gain_hbm,
     vert_hbm,
-    panel_ref,
-    side_ref,
-    flip_ref,
+    panel_hbm,
+    side_hbm,
+    flip_hbm,
     spread,
     small_ref,
     inp,
+    tables,
     packed,
     st_row,
     st_col,
@@ -43,6 +44,7 @@
     ry_row,
     ry_col,
     in_sem,
+    table_sem,
     send_sem,
     nb_sem,
     corner_sem,
@@ -227,6 +229,12 @@
     ]
     for load in loads:
         load.start()
+    table_loads = [
+        pltpu.make_async_copy(source, tables.at[i], table_sem.at[i])
+        for i, source in enumerate((panel_hbm, side_hbm, flip_hbm))
+    ]
+    for load in table_loads:
+        load.start()
 
     barrier = pltpu.get_barrier_semaphore()
     expected = jnp.int32(0)
@@ -255,12 +263,9 @@
         code = jnp.zeros_like(lane)
         for p in range(panels):
             here = lane // levels == p
-            index = jnp.where(here, panel_ref[side, p] * levels + lane % levels, index)
-            code = jnp.where(here, flip_ref[side, p] * 4 + side_ref[side, p], code)
+            index = jnp.where(here, tables[0, side, p] * levels + lane % levels, index)
+            code = jnp.where(here, tables[2, side, p] * 4 + tables[1, side, p], code)
         return index, code
-
-    row_pick = pick_tables(tr)
-    col_pick = pick_tables(2 + tc)
 
     def pack(value):
         filler = jnp.zeros((rows, cols, LANES - panels * levels), jnp.float32)
@@ -434,6 +439,11 @@
 
     partial = fine(beside)
 
+    for load in table_loads:
+        load.wait()
+    row_pick = pick_tables(tr)
+    col_pick = pick_tables(2 + tc)
+
     def arrived(ref, sem):
         pltpu.make_async_copy(ref, ref, sem).wait()
 
@@ -717,14 +727,14 @@
         spread, small = pl.pallas_call(
             functools.partial(kernel, nr, nc),
             out_shape=(
-                jax.ShapeDtypeStruct((rows, tall, LANES), f32),
-                jax.ShapeDtypeStruct((rows // 2, height, LANES), f32),
+                pltpu.VMEM((rows, tall, LANES), f32),
+                pltpu.VMEM((rows // 2, height, LANES), f32),
             ),
-            in_specs=[pl.BlockSpec(memory_space=pl.ANY)] * 4
-            + [pl.BlockSpec(memory_space=pltpu.SMEM)] * 3,
+            in_specs=[pl.BlockSpec(memory_space=pl.ANY)] * 7,
             out_specs=(pl.BlockSpec(memory_space=pltpu.VMEM),) * 2,
             scratch_shapes=[
                 pltpu.VMEM((4, panels, rows, cols, levels), f32),
+                pltpu.SMEM((3,) + edge_panel.T.shape, jnp.int32),
                 pltpu.VMEM((3, rows, tall, LANES), f32),
                 pltpu.VMEM((3, k, 3, block, LANES), f32),
                 pltpu.VMEM((3, 3, block, LANES), f32),
@@ -738,6 +748,7 @@
                 pltpu.VMEM((2, 8, TILE, LANES), f32),
                 pltpu.VMEM((2, 8, TILE, LANES), f32),
                 pltpu.SemaphoreType.DMA((4,)),
+                pltpu.SemaphoreType.DMA((3,)),
                 pltpu.SemaphoreType.DMA((count,)),
                 pltpu.SemaphoreType.DMA((4,)),
                 pltpu.SemaphoreType.DMA((4,)),
@@ -748,6 +759,8 @@
             ],
             compiler_params=pltpu.CompilerParams(collective_id=0, has_side_effects=True),
         )(residual, density, gain, vertical, edge_panel.T, edge_side.T, edge_flip.T)
+        spread = pltpu.with_memory_space_constraint(spread, pltpu.VMEM)
+        small = pltpu.with_memory_space_constraint(small, pltpu.VMEM)
         return pl.pallas_call(
             unpack,
             out_shape=(

time: 19.1 us -> 16.9 us (0.88)
  Pallas kernels: 18.3 us -> 16.1 us
    pallas_call x1, Pallas kernels: 16.6 us -> 15.3 us  [shards(): pl.pallas_call(functools.partial(kernel, nr, nc), out_shape=(pltpu.VMEM((...]
    pallas_call x1, Pallas kernels: 1.67 us -> 0.87 us  [shards(): pl.pallas_call(unpack, out_shape=(jax.ShapeDtypeStruct(residual.shape, f3...]
where the time goes in v2:
time: 16.9 us; the launch traced here: 16.8 us
  Pallas kernels  16.1 us (95%)
  between operations  0.64 us (4%)
    pallas_call x1, Pallas kernels, shards(): pl.pallas_call(functools.partial(kernel, nr, nc), out_shape=(pltpu.VMEM((...  15.3 us
    pallas_call x1, Pallas kernels, shards(): pl.pallas_call(unpack, out_shape=(jax.ShapeDtypeStruct(residual.shape, f3...  0.87 us

profile of v2, /device:TPU:0, one launch (start us, length us, event | category | flops | bytes accessed | tf_op | source)
XLA Modules:
  0.0 16.8 jit_solution(14740744486872001876)
XLA Ops:
  0.6 15.3 %shard_map.86 = (f32[6,16,128]{2,1,0:T(8,128)S(1)}, f32[3,8,128]{2,1,0:T(8,128)S(1)}) custom-call(f32[6,6,12,16]{3,2,1,0:T(8,128)} %res_hbm.1, f32[6,6,12,16]{3,2,1,0:T(8,128)} %den_hbm.1, f32[6,6,12,16]{3,2,1,0:T(8,128)} %gain_hbm.1, f32[6,6,12,16]{3,2,1,0:T(8,128)} %vert_hbm.1, s32[4,6]{1,0:T(4,128)} %bitcast.3, s32[4,6]{1,0:T(4,128)} %bitcast.4, ...), custom_call_target="tpu_custom_call" | custom-call | tf_op jit(solution)/shard_map/pallas_call | solution.py:727
  15.9 0.9 %shard_map.87 = (f32[6,6,12,16]{3,2,1,0:T(8,128)}, f32[6,3,6,16]{3,2,1,0:T(8,128)}) custom-call(f32[6,16,128]{2,1,0:T(8,128)S(1)} %get-tuple-element.4.spread, f32[3,8,128]{2,1,0:T(8,128)S(1)} %get-tuple-element.5.small_ref), custom_call_target="tpu_custom_call" | custom-call | tf_op jit(solution)/shard_map/pallas_call | solution.py:764

commit v3 on v2

--- a/solution.py
+++ b/solution.py
@@ -109,116 +109,169 @@
                     found.append((ok, (r + dr, c + dc)))
         return found
 
-    def messages():
-        found = []
-        src_row = st_row.at[tr]
-        for f in range(2):
-            slot = 4 * f + tr
-            to = c if f == 0 else nc - 1 - c
-            for e in range(2):
-                found.append((is_row, (e * (nr - 1), to), src_row, rx_row.at[slot], row_sem))
-        for f in range(2):
-            slot = 4 * f + 2 + tc
-            g = col_segment(f)
-            for e in range(2):
-                found.append(
-                    (is_col, (g, e * (nc - 1)), st_col.at[tc], rx_col.at[slot], col_sem)
-                )
-                found.append(
-                    (
-                        is_col,
-                        (e * (nr - 1), g // k),
-                        st_col.at[tc],
-                        rx_row.at[slot, r % k],
-                        row_sem,
-                    )
-                )
-        for p in range(k):
-            for f in range(2):
-                slot = 4 * f + tr
-                g = row_segment(f, p)
-                for e in range(2):
-                    found.append(
-                        (is_row, (g, e * (nc - 1)), st_row.at[tr, p], rx_col.at[slot], col_sem)
-                    )
-        for h in range(2):
-            for f in range(2):
+    far_r, near_r = (1 - tr) * (nr - 1), tr * (nr - 1)
+    far_c, near_c = (1 - tc) * (nc - 1), tc * (nc - 1)
+    used = 6
+
+    def traffic(sending):
+        count = [0]
+
+        def remote(src, dst, sem, dest):
+            m = count[0]
+            count[0] += 1
+            if sending:
+                pltpu.make_async_remote_copy(
+                    src_ref=src,
+                    dst_ref=dst,
+                    send_sem=send_sem.at[m],
+                    recv_sem=sem,
+                    device_id=dest,
+                    device_id_type=MESH,
+                ).start()
+            else:
+                pltpu.make_async_copy(src, src, send_sem.at[m]).wait()
+
+        def local(src, dst, sem):
+            if sending:
+                pltpu.make_async_copy(src, dst, sem).start()
+
+        def either(src, dst, sem, dest, mine):
+            @pl.when(jnp.logical_not(mine))
+            def _():
+                remote(src, dst, sem, dest)
+
+            @pl.when(mine)
+            def _():
+                local(src, dst, sem)
+
+        @pl.when(is_row)
+        def _():
+            src = st_row.at[tr]
+            other = nc - 1 - c
+            remote(src, rx_row.at[4 + tr], row_sem, (far_r, other))
+            remote(src, rx_row.at[tr], row_sem, (far_r, c))
+            for p in range(k):
+                extreme = (c == 0) if p == 0 else (c == nc - 1)
+                if k == 1:
+                    extreme = extreme | (c == nc - 1)
+
+                def to_columns(p=p):
+                    for f in (1, 0):
+                        for ec in (far_c, near_c):
+                            remote(
+                                st_row.at[tr, p],
+                                rx_col.at[4 * f + tr],
+                                col_sem,
+                                (row_segment(f, p), ec),
+                            )
+
+                if 0 < p < k - 1:
+                    to_columns()
+                else:
+                    pl.when(jnp.logical_not(extreme))(to_columns)
+            remote(src, rx_row.at[4 + tr], row_sem, (near_r, other))
+            local(src, rx_row.at[tr], row_sem)
+
+        @pl.when(is_col)
+        def _():
+            src = st_col.at[tc]
+            for f in (1, 0):
+                dst = rx_row.at[4 * f + 2 + tc, r % k]
+                remote(src, dst, row_sem, (far_r, col_segment(f) // k))
+
+            @pl.when(jnp.logical_not(is_row))
+            def _():
+                remote(src, rx_col.at[6 + tc], col_sem, (nr - 1 - r, far_c))
+                remote(src, rx_col.at[6 + tc], col_sem, (nr - 1 - r, near_c))
+                remote(src, rx_col.at[2 + tc], col_sem, (r, far_c))
+                local(src, rx_col.at[2 + tc], col_sem)
+
+            for f in (1, 0):
+                dst = rx_row.at[4 * f + 2 + tc, r % k]
+                to = col_segment(f) // k
+                either(src, dst, row_sem, (near_r, to), is_row & (to == c))
+
+        for f in (1, 0):
+            for h in range(2):
                 d = 1 if h != f else -1
                 end = 0 if d == 1 else 1
-                for p in range(k):
+
+                @pl.when(is_row)
+                def _():
                     slot = 4 * f + tr
-                    src = ex_row.at[tr, p, h]
-                    to = row_segment(f, p) + d
-                    ok = is_row & (to >= 0) & (to < nr)
-                    for e in range(2):
-                        found.append(
-                            (
-                                ok,
-                                (clamp(to, nr), e * (nc - 1)),
-                                src,
-                                ry_col.at[end, slot],
-                                col_end_sem.at[end],
-                            )
-                        )
-                    if p == (k - 1 if h == 1 else 0):
-                        to = (c if f == 0 else nc - 1 - c) + d
-                        ok = is_row & (to >= 0) & (to < nc)
-                        for e in range(2):
-                            found.append(
-                                (
-                                    ok,
-                                    (e * (nr - 1), clamp(to, nc)),
-                                    src,
-                                    ry_row.at[end, slot],
-                                    row_end_sem.at[end],
-                                )
-                            )
-                slot = 4 * f + 2 + tc
-                src = ex_col.at[tc, h]
-                g = col_segment(f)
-                to = g + d
-                ok = is_col & (to >= 0) & (to < nr)
-                far = ok & (g % k == (k - 1 if d == 1 else 0))
-                for e in range(2):
-                    found.append(
-                        (ok, (clamp(to, nr), e * (nc - 1)), src, ry_col.at[end, slot], col_end_sem.at[end])
-                    )
-                    found.append(
-                        (
-                            far,
-                            (e * (nr - 1), clamp(g // k + d, nc)),
-                            src,
-                            ry_row.at[end, slot],
-                            row_end_sem.at[end],
-                        )
-                    )
-        border = len(found)
+                    for p in range(k):
+                        outer_end = p == (k - 1 if h == 1 else 0)
+
+                        def ends(p=p, outer_end=outer_end):
+                            src = ex_row.at[tr, p, h, 0:used]
+                            to = clamp(row_segment(f, p) + d, nr)
+                            dst = ry_col.at[end, slot, 0:used]
+                            sem = col_end_sem.at[end]
+                            remote(src, dst, sem, (to, far_c))
+                            either(src, dst, sem, (to, near_c), is_col & (to == r))
+                            if outer_end:
+                                to = clamp((c if f == 0 else nc - 1 - c) + d, nc)
+                                dst = ry_row.at[end, slot, 0:used]
+                                sem = row_end_sem.at[end]
+                                remote(src, dst, sem, (far_r, to))
+                                if f == 0:
+                                    remote(src, dst, sem, (near_r, to))
+                                else:
+                                    either(src, dst, sem, (near_r, to), to == c)
+
+                        if outer_end:
+                            pl.when(col_ok[h])(ends)
+                        else:
+                            ends()
+
+                @pl.when(is_col & row_ok[h])
+                def _():
+                    slot = 4 * f + 2 + tc
+                    src = ex_col.at[tc, h, 0:used]
+                    g = col_segment(f)
+                    to = clamp(g + d, nr)
+                    dst = ry_col.at[end, slot, 0:used]
+                    sem = col_end_sem.at[end]
+                    remote(src, dst, sem, (to, far_c))
+                    if f == 0:
+                        remote(src, dst, sem, (to, near_c))
+                    else:
+                        either(src, dst, sem, (to, near_c), to == r)
+
+                    def crossing():
+                        to = clamp(g // k + d, nc)
+                        dst = ry_row.at[end, slot, 0:used]
+                        sem = row_end_sem.at[end]
+                        remote(src, dst, sem, (far_r, to))
+                        either(src, dst, sem, (near_r, to), is_row & (to == c))
+
+                    if k == 1:
+                        crossing()
+                    else:
+                        pl.when(g % k == (k - 1 if d == 1 else 0))(crossing)
+
         for s in range(2):
-            found.append(
-                (row_ok[s], (r + 2 * s - 1, c), st_row.at[s], nb_row.at[1 - s], nb_sem.at[1 - s])
-            )
-            found.append(
-                (
-                    col_ok[s],
-                    (r, c + 2 * s - 1),
-                    st_col.at[s],
-                    nb_col.at[1 - s],
-                    nb_sem.at[3 - s],
-                )
-            )
+
+            @pl.when(row_ok[s])
+            def _():
+                remote(st_row.at[s], nb_row.at[1 - s], nb_sem.at[1 - s], (r + 2 * s - 1, c))
+
+            @pl.when(col_ok[s])
+            def _():
+                remote(st_col.at[s], nb_col.at[1 - s], nb_sem.at[3 - s], (r, c + 2 * s - 1))
+
         for s in range(2):
             for w in range(2):
                 at = 2 * (1 - s) + 1 - w
-                found.append(
-                    (
-                        row_ok[s] & col_ok[w],
+
+                @pl.when(row_ok[s] & col_ok[w])
+                def _():
+                    remote(
+                        ex_row.at[s, w * (k - 1), w, 0:used],
+                        corner.at[at, 0:used],
+                        corner_sem.at[at],
                         (r + 2 * s - 1, c + 2 * w - 1),
-                        ex_row.at[s, w * (k - 1), w],
-                        corner.at[at],
-                        corner_sem.at[at],
                     )
-                )
-        return found, border
 
     def same(dest):
         return (dest[0] == r) & (dest[1] == c)
@@ -406,27 +459,8 @@
             put(x, 4, at0(out[i0]))
             put(x, 5, at0(out[i1]))
 
-    sends, border = messages()
     pl.semaphore_wait(barrier, expected)
-    for m, (active, dest, src, dst, sem) in enumerate(sends):
-        mine = same(dest)
-
-        @pl.when(active & jnp.logical_not(mine) if m < border else active)
-        def _():
-            pltpu.make_async_remote_copy(
-                src_ref=src,
-                dst_ref=dst,
-                send_sem=send_sem.at[m],
-                recv_sem=sem,
-                device_id=dest,
-                device_id_type=MESH,
-            ).start()
-
-        if m < border:
-
-            @pl.when(active & mine)
-            def _():
-                pltpu.make_async_copy(src, dst, sem).start()
+    traffic(True)
 
     def beside(y, b):
         x = smoothed[y][b]
@@ -461,7 +495,7 @@
 
             @pl.when(row_ok[s] & col_ok[w])
             def _():
-                arrived(corner.at[2 * s + w], corner_sem.at[2 * s + w])
+                arrived(corner.at[2 * s + w, 0:used], corner_sem.at[2 * s + w])
 
     order = list(range(2 * length))[::-1] + [2 * length + 1, 2 * length]
     other = (
@@ -506,21 +540,36 @@
 
             @pl.when(col_ok[w])
             def _():
-                arrived(ry_row.at[w], row_end_sem.at[w])
+                arrived(ry_row.at[w, :, 0:used], row_end_sem.at[w])
                 read = lambda s: ry_row[w, s]
                 corner[2 * tr + w] = select(read, read, row_pick, None)
 
-    @pl.when(is_col)
+    @pl.when(is_col & jnp.logical_not(is_row))
     def _():
         arrived(rx_col, col_sem)
         for q in range(3):
             read = lambda s: rx_col[s, q]
             nb_col[tc, q] = select(read, read, col_pick, q)
+
+    @pl.when(is_col & is_row)
+    def _():
+        swap = (tr + tc) % 2
+        for q in range(3):
+
+            def read(s, q=q):
+                f, t = s // 4, s % 4
+                at = 4 * (1 - swap) + t if f == 1 else 4 * swap + t
+                return rx_row[at, (tr if f == 0 else 1 - tr) * (k - 1), q]
+
+            nb_col[tc, q] = select(read, read, col_pick, q)
+
+    @pl.when(is_col)
+    def _():
         for s in range(2):
 
             @pl.when(row_ok[s])
             def _():
-                arrived(ry_col.at[s], col_end_sem.at[s])
+                arrived(ry_col.at[s, :, 0:used], col_end_sem.at[s])
                 read = lambda slot: ry_col[s, slot]
                 value = select(read, read, col_pick, None)
                 corner[2 * s + tc, 0:2, :] = value[0:2]
@@ -695,11 +744,7 @@
             first = (2.0 - relaxation) * smoothed[y][b] + (1.0 - relaxation) * correction[i]
             spread[y, pl.ds(b, height, stride=2), :] = first + inverse[y][b] * total
 
-    for m, (active, dest, src, dst, sem) in enumerate(sends):
-
-        @pl.when(active & jnp.logical_not(same(dest)) if m < border else active)
-        def _():
-            pltpu.make_async_copy(src, src, send_sem.at[m]).wait()
+    traffic(False)
 
 
 def unpack(spread, small_ref, sol_ref, corr_ref):

time: 16.9 us -> 15.8 us (0.935)
  Pallas kernels: 16.1 us -> 15 us
    pallas_call x1, Pallas kernels: 15.3 us -> 14.1 us  [shards(): pl.pallas_call(functools.partial(kernel, nr, nc), out_shape=(pltpu.VMEM((...]
where the time goes in v3:
time: 15.8 us; the launch traced here: 15.6 us
  Pallas kernels  15 us (95%)
  between operations  0.64 us (4%)
    pallas_call x1, Pallas kernels, shards(): pl.pallas_call(functools.partial(kernel, nr, nc), out_shape=(pltpu.VMEM((...  14.1 us
    pallas_call x1, Pallas kernels, shards(): pl.pallas_call(unpack, out_shape=(jax.ShapeDtypeStruct(residual.shape, f3...  0.87 us

profile of v3, /device:TPU:0, one launch (start us, length us, event | category | flops | bytes accessed | tf_op | source)
XLA Modules:
  0.0 15.6 jit_solution(15101871932193952802)
XLA Ops:
  0.6 14.1 %shard_map.86 = (f32[6,16,128]{2,1,0:T(8,128)S(1)}, f32[3,8,128]{2,1,0:T(8,128)S(1)}) custom-call(f32[6,6,12,16]{3,2,1,0:T(8,128)} %res_hbm.1, f32[6,6,12,16]{3,2,1,0:T(8,128)} %den_hbm.1, f32[6,6,12,16]{3,2,1,0:T(8,128)} %gain_hbm.1, f32[6,6,12,16]{3,2,1,0:T(8,128)} %vert_hbm.1, s32[4,6]{1,0:T(4,128)} %bitcast.3, s32[4,6]{1,0:T(4,128)} %bitcast.4, ...), custom_call_target="tpu_custom_call" | custom-call | tf_op jit(solution)/shard_map/pallas_call | solution.py:772
  14.7 0.9 %shard_map.87 = (f32[6,6,12,16]{3,2,1,0:T(8,128)}, f32[6,3,6,16]{3,2,1,0:T(8,128)}) custom-call(f32[6,16,128]{2,1,0:T(8,128)S(1)} %get-tuple-element.4.spread, f32[3,8,128]{2,1,0:T(8,128)S(1)} %get-tuple-element.5.small_ref), custom_call_target="tpu_custom_call" | custom-call | tf_op jit(solution)/shard_map/pallas_call | solution.py:809

commit v4 on v3

--- a/solution.py
+++ b/solution.py
@@ -64,8 +64,8 @@
     c = lax.axis_index("ty")
     is_row = (r == 0) | (r == nr - 1)
     is_col = (c == 0) | (c == nc - 1)
-    tr = r // (nr - 1)
-    tc = c // (nc - 1)
+    tr = (r == nr - 1).astype(jnp.int32)
+    tc = (c == nc - 1).astype(jnp.int32)
     row_ok = (r > 0, r < nr - 1)
     col_ok = (c > 0, c < nc - 1)
 
@@ -78,39 +78,6 @@
     def clamp(x, n):
         return jnp.minimum(jnp.maximum(x, 0), n - 1)
 
-    def partners():
-        found = []
-        for f in range(2):
-            here = c if f == 0 else nc - 1 - c
-            for e in range(2):
-                for d in (-1, 0, 1):
-                    to = here + d
-                    found.append((is_row & (to >= 0) & (to < nc), (e * (nr - 1), clamp(to, nc))))
-                low = row_segment(f, 0 if f == 0 else k - 1)
-                for d in range(-1, k + 1):
-                    to = low + d
-                    found.append((is_row & (to >= 0) & (to < nr), (clamp(to, nr), e * (nc - 1))))
-                g = col_segment(f)
-                for d in (-1, 0, 1):
-                    to = g + d
-                    inside = is_col & (to >= 0) & (to < nr)
-                    found.append((inside, (clamp(to, nr), e * (nc - 1))))
-                    if d:
-                        inside = inside & (g % k == (k - 1 if d == 1 else 0))
-                    found.append((inside, (e * (nr - 1), clamp(g // k + d, nc))))
-        for dr in (-1, 0, 1):
-            for dc in (-1, 0, 1):
-                if dr or dc:
-                    ok = True
-                    if dr:
-                        ok = row_ok[(dr + 1) // 2]
-                    if dc:
-                        ok = col_ok[(dc + 1) // 2] if ok is True else ok & col_ok[(dc + 1) // 2]
-                    found.append((ok, (r + dr, c + dc)))
-        return found
-
-    far_r, near_r = (1 - tr) * (nr - 1), tr * (nr - 1)
-    far_c, near_c = (1 - tc) * (nc - 1), tc * (nc - 1)
     used = 6
 
     def traffic(sending):
@@ -144,114 +111,112 @@
             def _():
                 local(src, dst, sem)
 
-        @pl.when(is_row)
-        def _():
-            src = st_row.at[tr]
-            other = nc - 1 - c
-            remote(src, rx_row.at[4 + tr], row_sem, (far_r, other))
-            remote(src, rx_row.at[tr], row_sem, (far_r, c))
-            for p in range(k):
-                extreme = (c == 0) if p == 0 else (c == nc - 1)
-                if k == 1:
-                    extreme = extreme | (c == nc - 1)
-
-                def to_columns(p=p):
-                    for f in (1, 0):
-                        for ec in (far_c, near_c):
-                            remote(
-                                st_row.at[tr, p],
-                                rx_col.at[4 * f + tr],
-                                col_sem,
-                                (row_segment(f, p), ec),
-                            )
-
-                if 0 < p < k - 1:
-                    to_columns()
-                else:
-                    pl.when(jnp.logical_not(extreme))(to_columns)
-            remote(src, rx_row.at[4 + tr], row_sem, (near_r, other))
-            local(src, rx_row.at[tr], row_sem)
-
-        @pl.when(is_col)
-        def _():
-            src = st_col.at[tc]
+        def at_row(e):
+            return r == e * (nr - 1)
+
+        def at_col(e):
+            return c == e * (nc - 1)
+
+        def strips_to_rows(e):
+            row = e * (nr - 1)
+
+            @pl.when(is_row)
+            def _():
+                src = st_row.at[tr]
+                remote(src, rx_row.at[4 + tr], row_sem, (row, nc - 1 - c))
+                either(src, rx_row.at[tr], row_sem, (row, c), at_row(e))
+
+            @pl.when(is_col)
+            def _():
+                for f in (1, 0):
+                    dst = rx_row.at[4 * f + 2 + tc, lax.rem(r, k)]
+                    to = lax.div(col_segment(f), k)
+                    either(st_col.at[tc], dst, row_sem, (row, to), at_row(e) & (to == c))
+
+        def strips_to_columns(e):
+            col = e * (nc - 1)
+
+            @pl.when(is_row)
+            def _():
+                for p in range(k):
+                    extreme = (c == 0) if p == 0 else (c == nc - 1)
+                    if k == 1:
+                        extreme = extreme | (c == nc - 1)
+
+                    def to_columns(p=p):
+                        for f in (1, 0):
+                            to = row_segment(f, p)
+                            remote(st_row.at[tr, p], rx_col.at[4 * f + tr], col_sem, (to, col))
+
+                    if 0 < p < k - 1:
+                        to_columns()
+                    else:
+                        pl.when(jnp.logical_not(extreme))(to_columns)
+
+            @pl.when(is_col & jnp.logical_not(is_row))
+            def _():
+                src = st_col.at[tc]
+                remote(src, rx_col.at[6 + tc], col_sem, (nr - 1 - r, col))
+                either(src, rx_col.at[2 + tc], col_sem, (r, col), at_col(e))
+
+        def ends(e):
+            row, col = e * (nr - 1), e * (nc - 1)
             for f in (1, 0):
-                dst = rx_row.at[4 * f + 2 + tc, r % k]
-                remote(src, dst, row_sem, (far_r, col_segment(f) // k))
-
-            @pl.when(jnp.logical_not(is_row))
-            def _():
-                remote(src, rx_col.at[6 + tc], col_sem, (nr - 1 - r, far_c))
-                remote(src, rx_col.at[6 + tc], col_sem, (nr - 1 - r, near_c))
-                remote(src, rx_col.at[2 + tc], col_sem, (r, far_c))
-                local(src, rx_col.at[2 + tc], col_sem)
-
-            for f in (1, 0):
-                dst = rx_row.at[4 * f + 2 + tc, r % k]
-                to = col_segment(f) // k
-                either(src, dst, row_sem, (near_r, to), is_row & (to == c))
-
-        for f in (1, 0):
-            for h in range(2):
-                d = 1 if h != f else -1
-                end = 0 if d == 1 else 1
-
-                @pl.when(is_row)
-                def _():
-                    slot = 4 * f + tr
-                    for p in range(k):
-                        outer_end = p == (k - 1 if h == 1 else 0)
-
-                        def ends(p=p, outer_end=outer_end):
-                            src = ex_row.at[tr, p, h, 0:used]
-                            to = clamp(row_segment(f, p) + d, nr)
-                            dst = ry_col.at[end, slot, 0:used]
-                            sem = col_end_sem.at[end]
-                            remote(src, dst, sem, (to, far_c))
-                            either(src, dst, sem, (to, near_c), is_col & (to == r))
+                for h in range(2):
+                    d = 1 if h != f else -1
+                    end = 0 if d == 1 else 1
+
+                    @pl.when(is_row)
+                    def _():
+                        slot = 4 * f + tr
+                        for p in range(k):
+                            outer_end = p == (k - 1 if h == 1 else 0)
+
+                            def one_end(p=p, outer_end=outer_end):
+                                src = ex_row.at[tr, p, h, 0:used]
+                                if outer_end:
+                                    to = clamp((c if f == 0 else nc - 1 - c) + d, nc)
+                                    dst = ry_row.at[end, slot, 0:used]
+                                    sem = row_end_sem.at[end]
+                                    if f == 0:
+                                        remote(src, dst, sem, (row, to))
+                                    else:
+                                        either(src, dst, sem, (row, to), at_row(e) & (to == c))
+                                to = clamp(row_segment(f, p) + d, nr)
+                                dst = ry_col.at[end, slot, 0:used]
+                                sem = col_end_sem.at[end]
+                                either(src, dst, sem, (to, col), at_col(e) & (to == r))
+
                             if outer_end:
-                                to = clamp((c if f == 0 else nc - 1 - c) + d, nc)
-                                dst = ry_row.at[end, slot, 0:used]
-                                sem = row_end_sem.at[end]
-                                remote(src, dst, sem, (far_r, to))
-                                if f == 0:
-                                    remote(src, dst, sem, (near_r, to))
-                                else:
-                                    either(src, dst, sem, (near_r, to), to == c)
-
-                        if outer_end:
-                            pl.when(col_ok[h])(ends)
+                                pl.when(col_ok[h])(one_end)
+                            else:
+                                one_end()
+
+                    @pl.when(is_col & row_ok[h])
+                    def _():
+                        slot = 4 * f + 2 + tc
+                        src = ex_col.at[tc, h, 0:used]
+                        g = col_segment(f)
+
+                        def crossing():
+                            to = clamp(lax.div(g, k) + d, nc)
+                            dst = ry_row.at[end, slot, 0:used]
+                            sem = row_end_sem.at[end]
+                            either(src, dst, sem, (row, to), at_row(e) & (to == c))
+
+                        if k == 1:
+                            crossing()
                         else:
-                            ends()
-
-                @pl.when(is_col & row_ok[h])
-                def _():
-                    slot = 4 * f + 2 + tc
-                    src = ex_col.at[tc, h, 0:used]
-                    g = col_segment(f)
-                    to = clamp(g + d, nr)
-                    dst = ry_col.at[end, slot, 0:used]
-                    sem = col_end_sem.at[end]
-                    remote(src, dst, sem, (to, far_c))
-                    if f == 0:
-                        remote(src, dst, sem, (to, near_c))
-                    else:
-                        either(src, dst, sem, (to, near_c), to == r)
-
-                    def crossing():
-                        to = clamp(g // k + d, nc)
-                        dst = ry_row.at[end, slot, 0:used]
-                        sem = row_end_sem.at[end]
-                        remote(src, dst, sem, (far_r, to))
-                        either(src, dst, sem, (near_r, to), is_row & (to == c))
-
-                    if k == 1:
-                        crossing()
-                    else:
-                        pl.when(g % k == (k - 1 if d == 1 else 0))(crossing)
-
-        for s in range(2):
-
+                            pl.when(lax.rem(g, k) == (k - 1 if d == 1 else 0))(crossing)
+                        to = clamp(g + d, nr)
+                        dst = ry_col.at[end, slot, 0:used]
+                        sem = col_end_sem.at[end]
+                        if f == 0:
+                            remote(src, dst, sem, (to, col))
+                        else:
+                            either(src, dst, sem, (to, col), at_col(e) & (to == r))
+
+        def within(s):
             @pl.when(row_ok[s])
             def _():
                 remote(st_row.at[s], nb_row.at[1 - s], nb_sem.at[1 - s], (r + 2 * s - 1, c))
@@ -260,7 +225,6 @@
             def _():
                 remote(st_col.at[s], nb_col.at[1 - s], nb_sem.at[3 - s], (r, c + 2 * s - 1))
 
-        for s in range(2):
             for w in range(2):
                 at = 2 * (1 - s) + 1 - w
 
@@ -273,8 +237,14 @@
                         (r + 2 * s - 1, c + 2 * w - 1),
                     )
 
-    def same(dest):
-        return (dest[0] == r) & (dest[1] == c)
+        within(0)
+        strips_to_rows(0)
+        ends(0)
+        strips_to_columns(0)
+        strips_to_rows(1)
+        ends(1)
+        strips_to_columns(1)
+        within(1)
 
     loads = [
         pltpu.make_async_copy(source, inp.at[i], in_sem.at[i])
@@ -290,14 +260,93 @@
         load.start()
 
     barrier = pltpu.get_barrier_semaphore()
-    expected = jnp.int32(0)
-    for active, dest in partners():
-        go = active & jnp.logical_not(same(dest))
-        expected = expected + go.astype(jnp.int32)
-
-        @pl.when(go)
-        def _():
-            pl.semaphore_signal(barrier, inc=1, device_id=dest, device_id_type=MESH)
+    far_r, near_r = (1 - tr) * (nr - 1), tr * (nr - 1)
+    far_c, near_c = (1 - tc) * (nc - 1), tc * (nc - 1)
+
+    def greet(dest):
+        pl.semaphore_signal(barrier, inc=1, device_id=dest, device_id_type=MESH)
+
+    def number(flag):
+        return flag.astype(jnp.int32)
+
+    def row_greetings():
+        found = []
+        for near in (False, True):
+            for f in (1, 0):
+                here = c if f == 0 else nc - 1 - c
+                for d in (0, -1, 1):
+                    if near and f == 0 and d == 0:
+                        continue
+                    ok = None if d == 0 else (here > 0) if d == -1 else (here < nc - 1)
+                    mine = (here + d == c) if near and f == 1 and d else None
+                    found.append((ok, mine, (near_r if near else far_r, clamp(here + d, nc))))
+        for near in (False, True):
+            for f in (1, 0):
+                low = row_segment(f, 0 if f == 0 else k - 1)
+                for d in range(-1, k + 1):
+                    ok = None if 0 <= d < k else (low > 0) if d == -1 else (low + d < nr)
+                    mine = (is_col & (low + d == r)) if near else None
+                    found.append((ok, mine, (clamp(low + d, nr), near_c if near else far_c)))
+        return found
+
+    def col_greetings():
+        found = []
+        for near in (False, True):
+            for f in (1, 0):
+                g = col_segment(f)
+                for d in (0, -1, 1):
+                    inside = None if d == 0 else (g > 0) if d == -1 else (g < nr - 1)
+                    if not (near and f == 0 and d == 0):
+                        mine = (g + d == r) if near and f == 1 and d else None
+                        found.append((inside, mine, (clamp(g + d, nr), near_c if near else far_c)))
+                    cross = inside
+                    if d and k > 1:
+                        cross = inside & (lax.rem(g, k) == (k - 1 if d == 1 else 0))
+                    to = lax.div(g, k) + d
+                    mine = (is_row & (to == c)) if near else None
+                    found.append((cross, mine, (near_r if near else far_r, clamp(to, nc))))
+        return found
+
+    def near_greetings():
+        found = []
+        for dr in (-1, 0, 1):
+            for dc in (-1, 0, 1):
+                if dr or dc:
+                    ok = row_ok[(dr + 1) // 2] if dr else None
+                    if dc:
+                        side = col_ok[(dc + 1) // 2]
+                        ok = side if ok is None else ok & side
+                    found.append((ok, None, (r + dr, c + dc)))
+        return found
+
+    def announce(found):
+        total = jnp.int32(0)
+        for ok, mine, dest in found:
+            go = ok
+            if mine is not None:
+                go = jnp.logical_not(mine) if go is None else go & jnp.logical_not(mine)
+            if go is None:
+                total = total + 1
+            else:
+                total = total + number(go)
+        return total
+
+    def tell(found):
+        for ok, mine, dest in found:
+            go = ok
+            if mine is not None:
+                go = jnp.logical_not(mine) if go is None else go & jnp.logical_not(mine)
+            if go is None:
+                greet(dest)
+            else:
+                pl.when(go)(functools.partial(greet, dest))
+
+    pl.when(is_row)(lambda: tell(row_greetings()))
+    pl.when(is_col)(lambda: tell(col_greetings()))
+    tell(near_greetings())
+    expected = announce(near_greetings())
+    expected = expected + jnp.where(is_row, announce(row_greetings()), 0)
+    expected = expected + jnp.where(is_col, announce(col_greetings()), 0)
 
     lane = lax.broadcasted_iota(jnp.int32, (TILE, LANES), 1)
     sub = lax.broadcasted_iota(jnp.int32, (height, LANES), 0)
@@ -472,6 +521,7 @@
         return total
 
     partial = fine(beside)
+    traffic(False)
 
     for load in table_loads:
         load.wait()
@@ -553,7 +603,7 @@
 
     @pl.when(is_col & is_row)
     def _():
-        swap = (tr + tc) % 2
+        swap = (tr != tc).astype(jnp.int32)
         for q in range(3):
 
             def read(s, q=q):
@@ -743,8 +793,6 @@
             total = total + (left if b == 0 else right)[i]
             first = (2.0 - relaxation) * smoothed[y][b] + (1.0 - relaxation) * correction[i]
             spread[y, pl.ds(b, height, stride=2), :] = first + inverse[y][b] * total
-
-    traffic(False)
 
 
 def unpack(spread, small_ref, sol_ref, corr_ref):

time: 15.8 us -> 14.7 us (0.930)
  Pallas kernels: 15 us -> 13.9 us
    pallas_call x1, Pallas kernels: 14.1 us -> 13.1 us  [shards(): pl.pallas_call(functools.partial(kernel, nr, nc), out_shape=(pltpu.VMEM((...]
where the time goes in v4:
time: 14.7 us; the launch traced here: 14.6 us
  Pallas kernels  13.9 us (95%)
  between operations  0.64 us (4%)
    pallas_call x1, Pallas kernels, shards(): pl.pallas_call(functools.partial(kernel, nr, nc), out_shape=(pltpu.VMEM((...  13.1 us
    pallas_call x1, Pallas kernels, shards(): pl.pallas_call(unpack, out_shape=(jax.ShapeDtypeStruct(residual.shape, f3...  0.87 us

profile of v4, /device:TPU:0, one launch (start us, length us, event | category | flops | bytes accessed | tf_op | source)
XLA Modules:
  0.0 14.6 jit_solution(18383240276534119141)
XLA Ops:
  0.6 13.1 %shard_map.86 = (f32[6,16,128]{2,1,0:T(8,128)S(1)}, f32[3,8,128]{2,1,0:T(8,128)S(1)}) custom-call(f32[6,6,12,16]{3,2,1,0:T(8,128)} %res_hbm.1, f32[6,6,12,16]{3,2,1,0:T(8,128)} %den_hbm.1, f32[6,6,12,16]{3,2,1,0:T(8,128)} %gain_hbm.1, f32[6,6,12,16]{3,2,1,0:T(8,128)} %vert_hbm.1, s32[4,6]{1,0:T(4,128)} %bitcast.3, s32[4,6]{1,0:T(4,128)} %bitcast.4, ...), custom_call_target="tpu_custom_call" | custom-call | tf_op jit(solution)/shard_map/pallas_call | solution.py:820
  13.7 0.9 %shard_map.87 = (f32[6,6,12,16]{3,2,1,0:T(8,128)}, f32[6,3,6,16]{3,2,1,0:T(8,128)}) custom-call(f32[6,16,128]{2,1,0:T(8,128)S(1)} %get-tuple-element.4.spread, f32[3,8,128]{2,1,0:T(8,128)S(1)} %get-tuple-element.5.small_ref), custom_call_target="tpu_custom_call" | custom-call | tf_op jit(solution)/shard_map/pallas_call | solution.py:857

commit v5 on v4

--- a/solution.py
+++ b/solution.py
@@ -81,22 +81,18 @@
     used = 6
 
     def traffic(sending):
-        count = [0]
-
         def remote(src, dst, sem, dest):
-            m = count[0]
-            count[0] += 1
             if sending:
                 pltpu.make_async_remote_copy(
                     src_ref=src,
                     dst_ref=dst,
-                    send_sem=send_sem.at[m],
+                    send_sem=send_sem.at[0],
                     recv_sem=sem,
                     device_id=dest,
                     device_id_type=MESH,
                 ).start()
             else:
-                pltpu.make_async_copy(src, src, send_sem.at[m]).wait()
+                pltpu.make_async_copy(src, src, send_sem.at[0]).wait()
 
         def local(src, dst, sem):
             if sending:
@@ -237,17 +233,17 @@
                         (r + 2 * s - 1, c + 2 * w - 1),
                     )
 
+        strips_to_rows(0)
         within(0)
-        strips_to_rows(0)
         ends(0)
+        strips_to_rows(1)
         strips_to_columns(0)
-        strips_to_rows(1)
+        strips_to_columns(1)
         ends(1)
-        strips_to_columns(1)
         within(1)
 
     loads = [
-        pltpu.make_async_copy(source, inp.at[i], in_sem.at[i])
+        pltpu.make_async_copy(source, inp.at[i], in_sem.at[i // 2])
         for i, source in enumerate((gain_hbm, vert_hbm, den_hbm, res_hbm))
     ]
     for load in loads:
@@ -393,9 +389,8 @@
         y = 2 * i
         return 0.25 * (values[y][0] + values[y][1] + values[y + 1][0] + values[y + 1][1])
 
-    loads[0].wait()
+    pltpu.make_async_copy(inp.at[0:2], inp.at[0:2], in_sem.at[0]).wait()
     gain = split(1, pack(inp[0]))
-    loads[1].wait()
     vertical = split(2, pack(inp[1]))
     low_vert = fine(lambda y, b: lower(vertical[y][b]))
     inverse = fine(
@@ -404,8 +399,7 @@
     c_vert = [block_mean(vertical, i) for i in small]
     c_low = [lower(c_vert[i]) for i in small]
     c_inv = [relaxation / (block_mean(gain, i) + 1.0 + c_vert[i] + c_low[i]) for i in small]
-    loads[2].wait()
-    loads[3].wait()
+    pltpu.make_async_copy(inp.at[2:4], inp.at[2:4], in_sem.at[1]).wait()
     right_side = split(0, pack(inp[2] * inp[3]))
     smoothed = fine(lambda y, b: inverse[y][b] * right_side[y][b])
 
@@ -795,13 +789,22 @@
             spread[y, pl.ds(b, height, stride=2), :] = first + inverse[y][b] * total
 
 
-def unpack(spread, small_ref, sol_ref, corr_ref):
-    panels, _, cols, levels = sol_ref.shape
-    half_c = corr_ref.shape[2]
+def unpack(spread, small_ref, sol_hbm, corr_hbm, sol, corr, sem):
+    panels, _, cols, levels = sol.shape
+    half_c = corr.shape[2]
+    copies = []
     for p in range(panels):
         lanes = slice(p * levels, (p + 1) * levels)
-        sol_ref[p] = spread[:, :cols, lanes]
-        corr_ref[p] = small_ref[:, :half_c, lanes]
+        sol[p] = spread[:, :cols, lanes]
+        copies.append(pltpu.make_async_copy(sol.at[p], sol_hbm.at[p], sem.at[p]))
+        copies[-1].start()
+    for p in range(panels):
+        lanes = slice(p * levels, (p + 1) * levels)
+        corr[p] = small_ref[:, :half_c, lanes]
+    copies.append(pltpu.make_async_copy(corr, corr_hbm, sem.at[panels]))
+    copies[-1].start()
+    for copy in copies:
+        copy.wait()
 
 
 def solution(mesh):
@@ -816,7 +819,6 @@
         height = round_up(cols // 2, TILE)
         tall = 2 * height
         f32 = jnp.float32
-        count = 4 + 8 + 4 * k + 8 * k + 8 + 16 + 4 + 4
         spread, small = pl.pallas_call(
             functools.partial(kernel, nr, nc),
             out_shape=(
@@ -840,9 +842,9 @@
                 pltpu.VMEM((8, 3, block, LANES), f32),
                 pltpu.VMEM((2, 8, TILE, LANES), f32),
                 pltpu.VMEM((2, 8, TILE, LANES), f32),
-                pltpu.SemaphoreType.DMA((4,)),
+                pltpu.SemaphoreType.DMA((2,)),
                 pltpu.SemaphoreType.DMA((3,)),
-                pltpu.SemaphoreType.DMA((count,)),
+                pltpu.SemaphoreType.DMA((1,)),
                 pltpu.SemaphoreType.DMA((4,)),
                 pltpu.SemaphoreType.DMA((4,)),
                 pltpu.SemaphoreType.DMA,
@@ -861,7 +863,12 @@
                 jax.ShapeDtypeStruct((panels, rows // 2, cols // 2, levels), f32),
             ),
             in_specs=[pl.BlockSpec(memory_space=pltpu.VMEM)] * 2,
-            out_specs=(pl.BlockSpec(memory_space=pltpu.VMEM),) * 2,
+            out_specs=(pl.BlockSpec(memory_space=pl.ANY),) * 2,
+            scratch_shapes=[
+                pltpu.VMEM(residual.shape, f32),
+                pltpu.VMEM((panels, rows // 2, cols // 2, levels), f32),
+                pltpu.SemaphoreType.DMA((panels + 1,)),
+            ],
         )(spread, small)
 
     fields = P(None, "tx", "ty", None)

time: 14.7 us -> 14 us (0.952)
  Pallas kernels: 13.9 us -> 13.2 us
    pallas_call x1, Pallas kernels: 13.1 us -> 12.4 us  [shards(): pl.pallas_call(functools.partial(kernel, nr, nc), out_shape=(pltpu.VMEM((...]
where the time goes in v5:
time: 14 us; the launch traced here: 13.9 us
  Pallas kernels  13.2 us (94%)
  between operations  0.64 us (5%)
    pallas_call x1, Pallas kernels, shards(): pl.pallas_call(functools.partial(kernel, nr, nc), out_shape=(pltpu.VMEM((...  12.4 us
    pallas_call x1, Pallas kernels, shards(): pl.pallas_call(unpack, out_shape=(jax.ShapeDtypeStruct(residual.shape, f3...  0.83 us

profile of v5, /device:TPU:0, one launch (start us, length us, event | category | flops | bytes accessed | tf_op | source)
XLA Modules:
  0.0 13.9 jit_solution(14288432680648955905)
XLA Ops:
  0.6 12.4 %shard_map.86 = (f32[6,16,128]{2,1,0:T(8,128)S(1)}, f32[3,8,128]{2,1,0:T(8,128)S(1)}) custom-call(f32[6,6,12,16]{3,2,1,0:T(8,128)} %res_hbm.1, f32[6,6,12,16]{3,2,1,0:T(8,128)} %den_hbm.1, f32[6,6,12,16]{3,2,1,0:T(8,128)} %gain_hbm.1, f32[6,6,12,16]{3,2,1,0:T(8,128)} %vert_hbm.1, s32[4,6]{1,0:T(4,128)} %bitcast.3, s32[4,6]{1,0:T(4,128)} %bitcast.4, ...), custom_call_target="tpu_custom_call" | custom-call | tf_op jit(solution)/shard_map/pallas_call | solution.py:822
  13.0 0.8 %shard_map.87 = (f32[6,6,12,16]{3,2,1,0:T(8,128)}, f32[6,3,6,16]{3,2,1,0:T(8,128)}) custom-call(f32[6,16,128]{2,1,0:T(8,128)S(1)} %get-tuple-element.4.spread, f32[3,8,128]{2,1,0:T(8,128)S(1)} %get-tuple-element.5.small_ref), custom_call_target="tpu_custom_call" | custom-call | tf_op jit(solution)/shard_map/pallas_call | solution.py:859

commit v6 on v5

--- a/solution.py
+++ b/solution.py
@@ -34,6 +34,8 @@
     packed,
     st_row,
     st_col,
+    sp_row,
+    sp_col,
     ex_row,
     ex_col,
     nb_row,
@@ -79,6 +81,9 @@
         return jnp.minimum(jnp.maximum(x, 0), n - 1)
 
     used = 6
+    full = panels * levels
+    spare = LANES - full
+    packed_rows = 3 * rows
 
     def traffic(sending):
         def remote(src, dst, sem, dest):
@@ -118,16 +123,20 @@
 
             @pl.when(is_row)
             def _():
-                src = st_row.at[tr]
-                remote(src, rx_row.at[4 + tr], row_sem, (row, nc - 1 - c))
-                either(src, rx_row.at[tr], row_sem, (row, c), at_row(e))
+                src = sp_row.at[tr, :, 0:packed_rows]
+                to = jnp.minimum(c, nc - 1 - c)
+                f = (c > to).astype(jnp.int32)
+                for to, f in ((to, f), (nc - 1 - to, 1 - f)):
+                    either(src, rx_row.at[4 * f + tr, :, 0:packed_rows], row_sem, (row, to), at_row(e) & (to == c))
 
             @pl.when(is_col)
             def _():
-                for f in (1, 0):
-                    dst = rx_row.at[4 * f + 2 + tc, lax.rem(r, k)]
-                    to = lax.div(col_segment(f), k)
-                    either(st_col.at[tc], dst, row_sem, (row, to), at_row(e) & (to == c))
+                g = jnp.minimum(r, nr - 1 - r)
+                f = (r > g).astype(jnp.int32)
+                for g, f in ((g, f), (nr - 1 - g, 1 - f)):
+                    dst = rx_row.at[4 * f + 2 + tc, lax.rem(r, k), 0:packed_rows]
+                    to = lax.div(g, k)
+                    either(sp_col.at[tc, 0:packed_rows], dst, row_sem, (row, to), at_row(e) & (to == c))
 
         def strips_to_columns(e):
             col = e * (nc - 1)
@@ -234,6 +243,8 @@
                     )
 
         strips_to_rows(0)
+        if sending:
+            stage_ends()
         within(0)
         ends(0)
         strips_to_rows(1)
@@ -242,14 +253,13 @@
         ends(1)
         within(1)
 
-    loads = [
-        pltpu.make_async_copy(source, inp.at[i], in_sem.at[i // 2])
-        for i, source in enumerate((gain_hbm, vert_hbm, den_hbm, res_hbm))
-    ]
-    for load in loads:
-        load.start()
+    fields = (gain_hbm, vert_hbm, den_hbm, res_hbm)
+    for pair in range(2):
+        for p in range(panels):
+            for i in (2 * pair, 2 * pair + 1):
+                pltpu.make_async_copy(fields[i].at[p], inp.at[i, p], in_sem.at[pair]).start()
     table_loads = [
-        pltpu.make_async_copy(source, tables.at[i], table_sem.at[i])
+        pltpu.make_async_copy(source, tables.at[i], table_sem.at[0])
         for i, source in enumerate((panel_hbm, side_hbm, flip_hbm))
     ]
     for load in table_loads:
@@ -363,7 +373,8 @@
             here = lane // levels == p
             index = jnp.where(here, tables[0, side, p] * levels + lane % levels, index)
             code = jnp.where(here, tables[2, side, p] * 4 + tables[1, side, p], code)
-        return index, code
+        chunk = index // spare
+        return index, code, jnp.where(lane < full, full + index - chunk * spare, lane), chunk
 
     def pack(value):
         filler = jnp.zeros((rows, cols, LANES - panels * levels), jnp.float32)
@@ -440,6 +451,14 @@
 
     def put(ref, at, value):
         ref[at : at + value.shape[0], :] = value
+
+    def press(ref, runs, singles):
+        for at, run in enumerate(runs):
+            put(ref, at * length, run)
+        singles = jnp.concatenate(singles + [jnp.zeros((TILE - used, LANES), jnp.float32)], axis=0)
+        for j in range(full // spare):
+            moved = pltpu.roll(singles, full - spare * j, 1)
+            ref[used * j : used * (j + 1), full:] = moved[:used, full:]
 
     for s in range(2):
         y = s * (rows - 1)
@@ -462,16 +481,13 @@
             put(g, length, c_vert[i0][seg])
             put(g, 2 * length, one(west[i1], lo))
             put(g, 2 * length + 1, one(east[i1], hi))
-            for h in range(2):
-                j, j1 = (lo, lo + 1) if h == 0 else (hi, hi - 1)
-                side = west if h == 0 else east
-                x = ex_row.at[s, p, h]
-                put(x, 0, one(by_piece[i0], j))
-                put(x, 1, one(c_inv[i0], j))
-                put(x, 2, one(side[i0], j))
-                put(x, 3, one(side[i1], j))
-                put(x, 4, one(out, j))
-                put(x, 5, one(out, j1))
+            parts = (smoothed[y][0], smoothed[y][1], by_piece[i0], by_piece[i1])
+            press(
+                sp_row.at[s, p],
+                [x[seg] for x in parts + (c_inv[i0], c_vert[i0])],
+                [one(c_inv[i1], lo), one(c_inv[i1], hi)]
+                + [one(west[i0], lo), one(east[i0], hi), one(west[i1], lo), one(east[i1], hi)],
+            )
     for s in range(2):
         j0, j1 = (0, 1) if s == 0 else (half_c - 1, half_c - 2)
         out = west if s == 0 else east
@@ -491,16 +507,53 @@
         put(b, 2 * length + 1, at0(south[half_r - 1]))
         put(g, 2 * length, at1(north[0]))
         put(g, 2 * length + 1, at1(south[half_r - 1]))
-        for h in range(2):
-            i0, i1 = (0, 1) if h == 0 else (half_r - 1, half_r - 2)
-            side = north[0] if h == 0 else south[half_r - 1]
-            x = ex_col.at[s, h]
-            put(x, 0, at0(by_tile[i0]))
-            put(x, 1, at0(c_inv[i0]))
-            put(x, 2, at0(side))
-            put(x, 3, at1(side))
-            put(x, 4, at0(out[i0]))
-            put(x, 5, at0(out[i1]))
+        parts = [
+            [at0(smoothed[2 * i][s]) for i in small],
+            [at0(smoothed[2 * i + 1][s]) for i in small],
+            [at0(x) for x in by_tile],
+            [at1(x) for x in by_tile],
+            [at0(x) for x in c_inv],
+            [at0(x) for x in c_vert],
+        ]
+        press(
+            sp_col.at[s],
+            [jnp.concatenate(x, axis=0) for x in parts],
+            [at1(c_inv[0]), at1(c_inv[half_r - 1]), at0(north[0]), at0(south[half_r - 1])]
+            + [at1(north[0]), at1(south[half_r - 1])],
+        )
+
+    def stage_ends():
+        for s in range(2):
+            i0, i1 = (0, 1) if s == 0 else (half_r - 1, half_r - 2)
+            out = north[0] if s == 0 else south[half_r - 1]
+            for p in range(k):
+                lo, hi = p * length, p * length + last
+                one = lambda x, j: x[j : j + 1]
+                for h in range(2):
+                    j, j1 = (lo, lo + 1) if h == 0 else (hi, hi - 1)
+                    side = west if h == 0 else east
+                    x = ex_row.at[s, p, h]
+                    put(x, 0, one(by_piece[i0], j))
+                    put(x, 1, one(c_inv[i0], j))
+                    put(x, 2, one(side[i0], j))
+                    put(x, 3, one(side[i1], j))
+                    put(x, 4, one(out, j))
+                    put(x, 5, one(out, j1))
+        for s in range(2):
+            j0, j1 = (0, 1) if s == 0 else (half_c - 1, half_c - 2)
+            out = west if s == 0 else east
+            at0 = lambda x: x[j0 : j0 + 1]
+            at1 = lambda x: x[j1 : j1 + 1]
+            for h in range(2):
+                i0, i1 = (0, 1) if h == 0 else (half_r - 1, half_r - 2)
+                side = north[0] if h == 0 else south[half_r - 1]
+                x = ex_col.at[s, h]
+                put(x, 0, at0(by_tile[i0]))
+                put(x, 1, at0(c_inv[i0]))
+                put(x, 2, at0(side))
+                put(x, 3, at1(side))
+                put(x, 4, at0(out[i0]))
+                put(x, 5, at0(out[i1]))
 
     pl.semaphore_wait(barrier, expected)
     traffic(True)
@@ -517,8 +570,7 @@
     partial = fine(beside)
     traffic(False)
 
-    for load in table_loads:
-        load.wait()
+    pltpu.make_async_copy(tables, tables, table_sem.at[0]).wait()
     row_pick = pick_tables(tr)
     col_pick = pick_tables(2 + tc)
 
@@ -557,8 +609,8 @@
 
     flips = [flip_index(order), flip_index(other), flip_index(other)]
 
-    def choose(read, pick, f):
-        index, code = pick
+    def choose(read, pick, f, second=False):
+        index, code = pick[2 if second else 0], pick[1]
         taken = None
         for t in range(4):
             moved = jnp.take_along_axis(read(4 * f + t), index, axis=1, mode="promise_in_bounds")
@@ -572,14 +624,50 @@
             turned = jnp.take_along_axis(turned, flips[group], axis=0, mode="promise_in_bounds")
         return jnp.where(pick[1] >= 4, turned, straight)
 
+    def rows_of(tiles, first, final):
+        parts = []
+        for q, tile in enumerate(tiles):
+            lo, hi = max(first, q * TILE), min(final, (q + 1) * TILE)
+            if lo < hi:
+                parts.append(tile[lo - q * TILE : hi - q * TILE])
+        return parts
+
+    def select_packed(plainly, reverse, pick):
+        tiles = range(-(-packed_rows // TILE))
+        results = []
+        for f, read in ((0, plainly), (1, reverse)):
+            main = [choose(lambda s: read(s, q), pick, f) for q in tiles]
+            extra = [choose(lambda s: read(s, q), pick, f, True) for q in tiles]
+            singles = None
+            for j in range(full // spare):
+                part = jnp.concatenate(rows_of(extra, used * j, used * (j + 1)), axis=0)
+                same = pick[3][:used] == j
+                singles = part if singles is None else jnp.where(same, part, singles)
+            groups = []
+            for q in range(3):
+                lines = rows_of(main, 2 * length * q, 2 * length * (q + 1))
+                lines.append(singles[2 * q : 2 * q + 2])
+                if block > 2 * length + 2:
+                    lines.append(jnp.zeros((block - 2 * length - 2, LANES), jnp.float32))
+                groups.append(jnp.concatenate(lines, axis=0))
+            results.append(groups)
+        turned = [
+            jnp.take_along_axis(x, flips[q], axis=0, mode="promise_in_bounds")
+            for q, x in enumerate(results[1])
+        ]
+        return [jnp.where(pick[1] >= 4, x, y) for x, y in zip(turned, results[0])]
+
     @pl.when(is_row)
     def _():
-        arrived(rx_row, row_sem)
+        arrived(rx_row.at[:, :, 0:packed_rows], row_sem)
         for p in range(k):
+            value = select_packed(
+                lambda s, q: rx_row[s, p, q * TILE : (q + 1) * TILE],
+                lambda s, q: rx_row[s, k - 1 - p, q * TILE : (q + 1) * TILE],
+                row_pick,
+            )
             for q in range(3):
-                nb_row[tr, p, q] = select(
-                    lambda s: rx_row[s, p, q], lambda s: rx_row[s, k - 1 - p, q], row_pick, q
-                )
+                nb_row[tr, p, q] = value[q]
         for w in range(2):
 
             @pl.when(col_ok[w])
@@ -598,14 +686,16 @@
     @pl.when(is_col & is_row)
     def _():
         swap = (tr != tc).astype(jnp.int32)
+
+        def read(s, q):
+            f, t = s // 4, s % 4
+            at = 4 * (1 - swap) + t if f == 1 else 4 * swap + t
+            piece = (tr if f == 0 else 1 - tr) * (k - 1)
+            return rx_row[at, piece, q * TILE : (q + 1) * TILE]
+
+        value = select_packed(read, read, col_pick)
         for q in range(3):
-
-            def read(s, q=q):
-                f, t = s // 4, s % 4
-                at = 4 * (1 - swap) + t if f == 1 else 4 * swap + t
-                return rx_row[at, (tr if f == 0 else 1 - tr) * (k - 1), q]
-
-            nb_col[tc, q] = select(read, read, col_pick, q)
+            nb_col[tc, q] = value[q]
 
     @pl.when(is_col)
     def _():
@@ -792,19 +882,17 @@
 def unpack(spread, small_ref, sol_hbm, corr_hbm, sol, corr, sem):
     panels, _, cols, levels = sol.shape
     half_c = corr.shape[2]
-    copies = []
     for p in range(panels):
         lanes = slice(p * levels, (p + 1) * levels)
         sol[p] = spread[:, :cols, lanes]
-        copies.append(pltpu.make_async_copy(sol.at[p], sol_hbm.at[p], sem.at[p]))
-        copies[-1].start()
+        pltpu.make_async_copy(sol.at[p], sol_hbm.at[p], sem.at[0]).start()
     for p in range(panels):
         lanes = slice(p * levels, (p + 1) * levels)
         corr[p] = small_ref[:, :half_c, lanes]
-    copies.append(pltpu.make_async_copy(corr, corr_hbm, sem.at[panels]))
-    copies[-1].start()
-    for copy in copies:
-        copy.wait()
+    last = pltpu.make_async_copy(corr, corr_hbm, sem.at[1])
+    last.start()
+    pltpu.make_async_copy(sol, sol_hbm, sem.at[0]).wait()
+    last.wait()
 
 
 def solution(mesh):
@@ -816,6 +904,10 @@
         assert cols == k * rows and rows % 2 == 0 and panels * levels <= LANES
         assert rows >= 6 and nr > 1 and nc > 1
         block = round_up(rows + 2, TILE)
+        dense = round_up(3 * rows, TILE)
+        spare = LANES - panels * levels
+        assert spare % levels == 0 and panels * levels % spare == 0
+        assert 2 * panels * levels <= rows * spare
         height = round_up(cols // 2, TILE)
         tall = 2 * height
         f32 = jnp.float32
@@ -833,17 +925,19 @@
                 pltpu.VMEM((3, rows, tall, LANES), f32),
                 pltpu.VMEM((3, k, 3, block, LANES), f32),
                 pltpu.VMEM((3, 3, block, LANES), f32),
+                pltpu.VMEM((3, k, dense, LANES), f32),
+                pltpu.VMEM((3, dense, LANES), f32),
                 pltpu.VMEM((3, k, 2, TILE, LANES), f32),
                 pltpu.VMEM((3, 2, TILE, LANES), f32),
                 pltpu.VMEM((3, k, 3, block, LANES), f32),
                 pltpu.VMEM((3, 3, block, LANES), f32),
                 pltpu.VMEM((5, TILE, LANES), f32),
-                pltpu.VMEM((8, k, 3, block, LANES), f32),
+                pltpu.VMEM((8, k, dense, LANES), f32),
                 pltpu.VMEM((8, 3, block, LANES), f32),
                 pltpu.VMEM((2, 8, TILE, LANES), f32),
                 pltpu.VMEM((2, 8, TILE, LANES), f32),
                 pltpu.SemaphoreType.DMA((2,)),
-                pltpu.SemaphoreType.DMA((3,)),
+                pltpu.SemaphoreType.DMA((1,)),
                 pltpu.SemaphoreType.DMA((1,)),
                 pltpu.SemaphoreType.DMA((4,)),
                 pltpu.SemaphoreType.DMA((4,)),
@@ -867,7 +961,7 @@
             scratch_shapes=[
                 pltpu.VMEM(residual.shape, f32),
                 pltpu.VMEM((panels, rows // 2, cols // 2, levels), f32),
-                pltpu.SemaphoreType.DMA((panels + 1,)),
+                pltpu.SemaphoreType.DMA((2,)),
             ],
         )(spread, small)
 

time: 14 us -> 13.6 us (0.971)
  Pallas kernels: 13.2 us -> 12.8 us
    pallas_call x1, Pallas kernels: 12.4 us -> 12 us  [shards(): pl.pallas_call(functools.partial(kernel, nr, nc), out_shape=(pltpu.VMEM((...]
where the time goes in v6:
time: 13.6 us; the launch traced here: 13.4 us
  Pallas kernels  12.8 us (94%)
  between operations  0.64 us (5%)
    pallas_call x1, Pallas kernels, shards(): pl.pallas_call(functools.partial(kernel, nr, nc), out_shape=(pltpu.VMEM((...  12 us
    pallas_call x1, Pallas kernels, shards(): pl.pallas_call(unpack, out_shape=(jax.ShapeDtypeStruct(residual.shape, f3...  0.79 us

profile of v6, /device:TPU:0, one launch (start us, length us, event | category | flops | bytes accessed | tf_op | source)
XLA Modules:
  0.0 13.4 jit_solution(1065339290963135614)
XLA Ops:
  0.6 12.0 %shard_map.86 = (f32[6,16,128]{2,1,0:T(8,128)S(1)}, f32[3,8,128]{2,1,0:T(8,128)S(1)}) custom-call(f32[6,6,12,16]{3,2,1,0:T(8,128)} %res_hbm.1, f32[6,6,12,16]{3,2,1,0:T(8,128)} %den_hbm.1, f32[6,6,12,16]{3,2,1,0:T(8,128)} %gain_hbm.1, f32[6,6,12,16]{3,2,1,0:T(8,128)} %vert_hbm.1, s32[4,6]{1,0:T(4,128)} %bitcast.3, s32[4,6]{1,0:T(4,128)} %bitcast.4, ...), custom_call_target="tpu_custom_call" | custom-call | tf_op jit(solution)/shard_map/pallas_call | solution.py:914
  12.6 0.8 %shard_map.87 = (f32[6,6,12,16]{3,2,1,0:T(8,128)}, f32[6,3,6,16]{3,2,1,0:T(8,128)}) custom-call(f32[6,16,128]{2,1,0:T(8,128)S(1)} %get-tuple-element.4.spread, f32[3,8,128]{2,1,0:T(8,128)S(1)} %get-tuple-element.5.small_ref), custom_call_target="tpu_custom_call" | custom-call | tf_op jit(solution)/shard_map/pallas_call | solution.py:953

commit v7 on v6

--- a/solution.py
+++ b/solution.py
@@ -245,8 +245,8 @@
         strips_to_rows(0)
         if sending:
             stage_ends()
+        ends(0)
         within(0)
-        ends(0)
         strips_to_rows(1)
         strips_to_columns(0)
         strips_to_columns(1)
@@ -286,10 +286,10 @@
                     ok = None if d == 0 else (here > 0) if d == -1 else (here < nc - 1)
                     mine = (here + d == c) if near and f == 1 and d else None
                     found.append((ok, mine, (near_r if near else far_r, clamp(here + d, nc))))
-        for near in (False, True):
+        for d in range(-1, k + 1):
             for f in (1, 0):
                 low = row_segment(f, 0 if f == 0 else k - 1)
-                for d in range(-1, k + 1):
+                for near in (False, True):
                     ok = None if 0 <= d < k else (low > 0) if d == -1 else (low + d < nr)
                     mine = (is_col & (low + d == r)) if near else None
                     found.append((ok, mine, (clamp(low + d, nr), near_c if near else far_c)))
@@ -577,22 +577,6 @@
     def arrived(ref, sem):
         pltpu.make_async_copy(ref, ref, sem).wait()
 
-    for s in range(2):
-
-        @pl.when(row_ok[s])
-        def _():
-            arrived(nb_row.at[s], nb_sem.at[s])
-
-        @pl.when(col_ok[s])
-        def _():
-            arrived(nb_col.at[s], nb_sem.at[2 + s])
-
-        for w in range(2):
-
-            @pl.when(row_ok[s] & col_ok[w])
-            def _():
-                arrived(corner.at[2 * s + w, 0:used], corner_sem.at[2 * s + w])
-
     order = list(range(2 * length))[::-1] + [2 * length + 1, 2 * length]
     other = (
         list(range(length))[::-1]
@@ -709,6 +693,22 @@
                 corner[2 * s + tc, 0:2, :] = value[0:2]
                 corner[2 * s + tc, 2:4, :] = value[4:6]
                 corner[2 * s + tc, 4:6, :] = value[2:4]
+
+    for s in range(2):
+
+        @pl.when(row_ok[s])
+        def _():
+            arrived(nb_row.at[s], nb_sem.at[s])
+
+        @pl.when(col_ok[s])
+        def _():
+            arrived(nb_col.at[s], nb_sem.at[2 + s])
+
+        for w in range(2):
+
+            @pl.when(row_ok[s] & col_ok[w])
+            def _():
+                arrived(corner.at[2 * s + w, 0:used], corner_sem.at[2 * s + w])
 
     @pl.when(is_row & is_col)
     def _():

time: 13.6 us -> 13.3 us (0.978)
  Pallas kernels: 12.8 us -> 12.4 us
    pallas_call x1, Pallas kernels: 12 us -> 11.6 us  [shards(): pl.pallas_call(functools.partial(kernel, nr, nc), out_shape=(pltpu.VMEM((...]
where the time goes in v7:
time: 13.3 us; the launch traced here: 13.1 us
  Pallas kernels  12.4 us (93%)
  between operations  0.64 us (5%)
    pallas_call x1, Pallas kernels, shards(): pl.pallas_call(functools.partial(kernel, nr, nc), out_shape=(pltpu.VMEM((...  11.6 us
    pallas_call x1, Pallas kernels, shards(): pl.pallas_call(unpack, out_shape=(jax.ShapeDtypeStruct(residual.shape, f3...  0.79 us

profile of v7, /device:TPU:0, one launch (start us, length us, event | category | flops | bytes accessed | tf_op | source)
XLA Modules:
  0.0 13.1 jit_solution(7289569652301247597)
XLA Ops:
  0.6 11.6 %shard_map.86 = (f32[6,16,128]{2,1,0:T(8,128)S(1)}, f32[3,8,128]{2,1,0:T(8,128)S(1)}) custom-call(f32[6,6,12,16]{3,2,1,0:T(8,128)} %res_hbm.1, f32[6,6,12,16]{3,2,1,0:T(8,128)} %den_hbm.1, f32[6,6,12,16]{3,2,1,0:T(8,128)} %gain_hbm.1, f32[6,6,12,16]{3,2,1,0:T(8,128)} %vert_hbm.1, s32[4,6]{1,0:T(4,128)} %bitcast.3, s32[4,6]{1,0:T(4,128)} %bitcast.4, ...), custom_call_target="tpu_custom_call" | custom-call | tf_op jit(solution)/shard_map/pallas_call | solution.py:914
  12.3 0.8 %shard_map.87 = (f32[6,6,12,16]{3,2,1,0:T(8,128)}, f32[6,3,6,16]{3,2,1,0:T(8,128)}) custom-call(f32[6,16,128]{2,1,0:T(8,128)S(1)} %get-tuple-element.4.spread, f32[3,8,128]{2,1,0:T(8,128)S(1)} %get-tuple-element.5.small_ref), custom_call_target="tpu_custom_call" | custom-call | tf_op jit(solution)/shard_map/pallas_call | solution.py:953

commit v8 on v7

--- a/solution.py
+++ b/solution.py
@@ -245,6 +245,7 @@
         strips_to_rows(0)
         if sending:
             stage_ends()
+            stage_strips()
         ends(0)
         within(0)
         strips_to_rows(1)
@@ -468,19 +469,6 @@
             lo, hi = p * length, p * length + last
             seg = slice(lo, hi + 1)
             one = lambda x, j: x[j : j + 1]
-            a, b, g = (st_row.at[s, p, q] for q in range(3))
-            put(a, 0, smoothed[y][0][seg])
-            put(a, length, smoothed[y][1][seg])
-            put(a, 2 * length, one(c_inv[i1], lo))
-            put(a, 2 * length + 1, one(c_inv[i1], hi))
-            put(b, 0, by_piece[i0][seg])
-            put(b, length, by_piece[i1][seg])
-            put(b, 2 * length, one(west[i0], lo))
-            put(b, 2 * length + 1, one(east[i0], hi))
-            put(g, 0, c_inv[i0][seg])
-            put(g, length, c_vert[i0][seg])
-            put(g, 2 * length, one(west[i1], lo))
-            put(g, 2 * length + 1, one(east[i1], hi))
             parts = (smoothed[y][0], smoothed[y][1], by_piece[i0], by_piece[i1])
             press(
                 sp_row.at[s, p],
@@ -491,22 +479,8 @@
     for s in range(2):
         j0, j1 = (0, 1) if s == 0 else (half_c - 1, half_c - 2)
         out = west if s == 0 else east
-        a, b, g = (st_col.at[s, q] for q in range(3))
         at0 = lambda x: x[j0 : j0 + 1]
         at1 = lambda x: x[j1 : j1 + 1]
-        for y in range(rows):
-            put(a, (y % 2) * length + y // 2, at0(smoothed[y][s]))
-        put(a, 2 * length, at1(c_inv[0]))
-        put(a, 2 * length + 1, at1(c_inv[half_r - 1]))
-        for i in small:
-            put(b, i, at0(by_tile[i]))
-            put(b, length + i, at1(by_tile[i]))
-            put(g, i, at0(c_inv[i]))
-            put(g, length + i, at0(c_vert[i]))
-        put(b, 2 * length, at0(north[0]))
-        put(b, 2 * length + 1, at0(south[half_r - 1]))
-        put(g, 2 * length, at1(north[0]))
-        put(g, 2 * length + 1, at1(south[half_r - 1]))
         parts = [
             [at0(smoothed[2 * i][s]) for i in small],
             [at0(smoothed[2 * i + 1][s]) for i in small],
@@ -521,6 +495,48 @@
             [at1(c_inv[0]), at1(c_inv[half_r - 1]), at0(north[0]), at0(south[half_r - 1])]
             + [at1(north[0]), at1(south[half_r - 1])],
         )
+
+    def stage_strips():
+        for s in range(2):
+            y = s * (rows - 1)
+            i0, i1 = (0, 1) if s == 0 else (half_r - 1, half_r - 2)
+            out = north[0] if s == 0 else south[half_r - 1]
+            for p in range(k):
+                lo, hi = p * length, p * length + last
+                seg = slice(lo, hi + 1)
+                one = lambda x, j: x[j : j + 1]
+                a, b, g = (st_row.at[s, p, q] for q in range(3))
+                put(a, 0, smoothed[y][0][seg])
+                put(a, length, smoothed[y][1][seg])
+                put(a, 2 * length, one(c_inv[i1], lo))
+                put(a, 2 * length + 1, one(c_inv[i1], hi))
+                put(b, 0, by_piece[i0][seg])
+                put(b, length, by_piece[i1][seg])
+                put(b, 2 * length, one(west[i0], lo))
+                put(b, 2 * length + 1, one(east[i0], hi))
+                put(g, 0, c_inv[i0][seg])
+                put(g, length, c_vert[i0][seg])
+                put(g, 2 * length, one(west[i1], lo))
+                put(g, 2 * length + 1, one(east[i1], hi))
+        for s in range(2):
+            j0, j1 = (0, 1) if s == 0 else (half_c - 1, half_c - 2)
+            out = west if s == 0 else east
+            a, b, g = (st_col.at[s, q] for q in range(3))
+            at0 = lambda x: x[j0 : j0 + 1]
+            at1 = lambda x: x[j1 : j1 + 1]
+            for y in range(rows):
+                put(a, (y % 2) * length + y // 2, at0(smoothed[y][s]))
+            put(a, 2 * length, at1(c_inv[0]))
+            put(a, 2 * length + 1, at1(c_inv[half_r - 1]))
+            for i in small:
+                put(b, i, at0(by_tile[i]))
+                put(b, length + i, at1(by_tile[i]))
+                put(g, i, at0(c_inv[i]))
+                put(g, length + i, at0(c_vert[i]))
+            put(b, 2 * length, at0(north[0]))
+            put(b, 2 * length + 1, at0(south[half_r - 1]))
+            put(g, 2 * length, at1(north[0]))
+            put(g, 2 * length + 1, at1(south[half_r - 1]))
 
     def stage_ends():
         for s in range(2):

time: 13.3 us -> 13.3 us (level)
  no operation moved by 1% of the time
where the time goes in v8:
time: 13.3 us; the launch traced here: 13.1 us
  Pallas kernels  12.4 us (93%)
  between operations  0.64 us (5%)
    pallas_call x1, Pallas kernels, shards(): pl.pallas_call(functools.partial(kernel, nr, nc), out_shape=(pltpu.VMEM((...  11.6 us
    pallas_call x1, Pallas kernels, shards(): pl.pallas_call(unpack, out_shape=(jax.ShapeDtypeStruct(residual.shape, f3...  0.79 us

profile of v8, /device:TPU:0, one launch (start us, length us, event | category | flops | bytes accessed | tf_op | source)
XLA Modules:
  0.0 13.1 jit_solution(497300673607784690)
XLA Ops:
  0.6 11.6 %shard_map.86 = (f32[6,16,128]{2,1,0:T(8,128)S(1)}, f32[3,8,128]{2,1,0:T(8,128)S(1)}) custom-call(f32[6,6,12,16]{3,2,1,0:T(8,128)} %res_hbm.1, f32[6,6,12,16]{3,2,1,0:T(8,128)} %den_hbm.1, f32[6,6,12,16]{3,2,1,0:T(8,128)} %gain_hbm.1, f32[6,6,12,16]{3,2,1,0:T(8,128)} %vert_hbm.1, s32[4,6]{1,0:T(4,128)} %bitcast.3, s32[4,6]{1,0:T(4,128)} %bitcast.4, ...), custom_call_target="tpu_custom_call" | custom-call | tf_op jit(solution)/shard_map/pallas_call | solution.py:930
  12.3 0.8 %shard_map.87 = (f32[6,6,12,16]{3,2,1,0:T(8,128)}, f32[6,3,6,16]{3,2,1,0:T(8,128)}) custom-call(f32[6,16,128]{2,1,0:T(8,128)S(1)} %get-tuple-element.4.spread, f32[3,8,128]{2,1,0:T(8,128)S(1)} %get-tuple-element.5.small_ref), custom_call_target="tpu_custom_call" | custom-call | tf_op jit(solution)/shard_map/pallas_call | solution.py:969

commit v9 on v7

--- a/solution.py
+++ b/solution.py
@@ -652,14 +652,6 @@
             )
             for q in range(3):
                 nb_row[tr, p, q] = value[q]
-        for w in range(2):
-
-            @pl.when(col_ok[w])
-            def _():
-                arrived(ry_row.at[w, :, 0:used], row_end_sem.at[w])
-                read = lambda s: ry_row[w, s]
-                corner[2 * tr + w] = select(read, read, row_pick, None)
-
     @pl.when(is_col & jnp.logical_not(is_row))
     def _():
         arrived(rx_col, col_sem)
@@ -680,6 +672,16 @@
         value = select_packed(read, read, col_pick)
         for q in range(3):
             nb_col[tc, q] = value[q]
+
+    @pl.when(is_row)
+    def _():
+        for w in range(2):
+
+            @pl.when(col_ok[w])
+            def _():
+                arrived(ry_row.at[w, :, 0:used], row_end_sem.at[w])
+                read = lambda s: ry_row[w, s]
+                corner[2 * tr + w] = select(read, read, row_pick, None)
 
     @pl.when(is_col)
     def _():

time: 13.3 us -> 13.2 us (level)
  no operation moved by 1% of the time
where the time goes in v9:
time: 13.2 us; the launch traced here: 13 us
  Pallas kernels  12.4 us (94%)
  between operations  0.64 us (5%)
    pallas_call x1, Pallas kernels, shards(): pl.pallas_call(functools.partial(kernel, nr, nc), out_shape=(pltpu.VMEM((...  11.6 us
    pallas_call x1, Pallas kernels, shards(): pl.pallas_call(unpack, out_shape=(jax.ShapeDtypeStruct(residual.shape, f3...  0.79 us

profile of v9, /device:TPU:0, one launch (start us, length us, event | category | flops | bytes accessed | tf_op | source)
XLA Modules:
  0.0 13.0 jit_solution(11902668332144482809)
XLA Ops:
  0.6 11.6 %shard_map.86 = (f32[6,16,128]{2,1,0:T(8,128)S(1)}, f32[3,8,128]{2,1,0:T(8,128)S(1)}) custom-call(f32[6,6,12,16]{3,2,1,0:T(8,128)} %res_hbm.1, f32[6,6,12,16]{3,2,1,0:T(8,128)} %den_hbm.1, f32[6,6,12,16]{3,2,1,0:T(8,128)} %gain_hbm.1, f32[6,6,12,16]{3,2,1,0:T(8,128)} %vert_hbm.1, s32[4,6]{1,0:T(4,128)} %bitcast.3, s32[4,6]{1,0:T(4,128)} %bitcast.4, ...), custom_call_target="tpu_custom_call" | custom-call | tf_op jit(solution)/shard_map/pallas_call | solution.py:916
  12.2 0.8 %shard_map.87 = (f32[6,6,12,16]{3,2,1,0:T(8,128)}, f32[6,3,6,16]{3,2,1,0:T(8,128)}) custom-call(f32[6,16,128]{2,1,0:T(8,128)S(1)} %get-tuple-element.4.spread, f32[3,8,128]{2,1,0:T(8,128)S(1)} %get-tuple-element.5.small_ref), custom_call_target="tpu_custom_call" | custom-call | tf_op jit(solution)/shard_map/pallas_call | solution.py:955
